TPU v7x, 256 devices: a whole 4x4x8 slice. The times are simulated.
256 devices in a mesh: grp: 16 (over y_lo, z), seq: 16 (over y_hi, x, core).
Axes of the slice: x: 4, y: 4 (y_hi: 2, y_lo: 2; y = y_hi * 2 + y_lo), z: 8, core: 2. Of those that a mesh axis runs over, the one named last changes fastest.
Arguments:
- query_rows: bfloat16 [131072, 1024], P(('grp', 'seq')), may hold values from -96 to 96
- key_rows: bfloat16 [131072, 1024], P(('grp', 'seq')), may hold values from -8 to 8
- value_rows: bfloat16 [131072, 1024], P(('grp', 'seq')), may hold values from -12 to 12
- grad_out: bfloat16 [131072, 1024], P(('grp', 'seq')), may hold values from -6 to 6
Outputs:
- attended: bfloat16 [131072, 1024], P(('grp', 'seq'))
- grad_query: bfloat16 [131072, 1024], P(('grp', 'seq'))
- grad_key: bfloat16 [131072, 1024], P(('grp', 'seq'))
- grad_value: bfloat16 [131072, 1024], P(('grp', 'seq'))
All inputs are finite; a program needn't handle non-finite values.
Results may differ from a plain program's by a relative error of at most 0.0051.
Values may be sent and summed in bfloat16 or wider, within the bound.
A program may use at most 128 MiB of HBM per device.

v0:
```python
import jax
import jax.numpy as jnp
from jax import lax
from jax.sharding import Mesh
from jax.sharding import PartitionSpec as P

HEAD_DIM = 128
NEAR = 256
POOL1 = 16
MERGE = 16
GRP = ("grp_0", "grp_1")
GRP_SEQ = ("grp_0", "grp_1", "seq")


NEG_FILL = -1e30


def extended_2(array, sides, width):
    edges = {}
    for axis, dim in sides:
        size, length = (lax.axis_size(axis), array.shape[dim])
        up = [(i, (i + 1) % size) for i in range(size - 1)]
        last = lax.slice_in_dim(array, length - width, length, axis=dim)
        first = lax.slice_in_dim(array, 0, width, axis=dim)
        edges[dim] = (
            lax.ppermute(last, axis, up),
            lax.ppermute(first, axis, [(b, a) for a, b in up]),
        )
    done = []
    for _, dim in sides:
        low, high = edges[dim]
        around = [(width, width) if d in done else (0, 0) for d in range(array.ndim)]
        array = jnp.concatenate([jnp.pad(low, around), array, jnp.pad(high, around)], axis=dim)
        done.append(dim)
    return array


def in_order(parts, dim):
    lengths = list(parts.shape[1:])
    lengths[dim] *= parts.shape[0]
    return jnp.moveaxis(parts, 0, dim).reshape(lengths)


def from_everyone(array, axis):
    copies = jnp.broadcast_to(array, (lax.axis_size(axis), *array.shape))
    return lax.all_to_all(copies, axis, split_axis=0, concat_axis=0, tiled=True)


def gather_directly(array, axis, dim):
    return in_order(from_everyone(array, axis), dim)


def from_behind(block, axis, distance):
    devices = range(lax.axis_size(axis))
    route = [(i - distance, i) for i in devices if i - distance in devices]
    return lax.ppermute(block, axis, route)


def own_block(parts, axes, sequence):
    lengths = [lax.axis_size(a) for a in axes]
    parts = parts.reshape(*lengths, *parts.shape[1:])
    parts = parts.transpose(*sequence, *range(len(axes), parts.ndim))
    parts = parts.reshape(-1, *parts.shape[len(axes) :])
    for k in sequence:
        parts = lax.psum_scatter(parts, axes[k], scatter_dimension=0, tiled=True)
    return parts[0]


def in_blocks(array, dim, size):
    lengths = array.shape
    parts = array.reshape(*lengths[:dim], size, lengths[dim] // size, *lengths[dim + 1 :])
    return jnp.moveaxis(parts, dim, 0)


def summed_rows(array, axes, sequence, dim):
    size = lax.axis_size(axes)
    return own_block(in_blocks(array, dim, size), axes, sequence)


def pool_rows(values, factor):
    groups = values.shape[-2] // factor
    shaped = values.reshape(values.shape[:-2] + (groups, factor, values.shape[-1]))
    return jnp.mean(shaped, axis=-2, dtype=jnp.float32)


def expand_rows(values, factor):
    spread = jnp.broadcast_to(
        values[..., :, None, :], values.shape[:-1] + (factor, values.shape[-1])
    )
    return spread.reshape(values.shape[:-2] + (values.shape[-2] * factor, values.shape[-1]))


def split_heads(rows, head_count):
    return rows.reshape(rows.shape[0], head_count, -1).transpose(1, 0, 2)


def join_heads(stacked):
    return stacked.transpose(1, 0, 2).reshape(stacked.shape[1], stacked.shape[0] * stacked.shape[2])


def head_pass(operands, bias_row, scaling):
    query_head, grad_head, key_head, value_head = operands
    scores = (
        jnp.einsum("qd,kd->qk", query_head, key_head, preferred_element_type=jnp.float32) * scaling
        + bias_row
    )
    weights = jax.nn.softmax(scores, axis=-1)
    rounded = weights.astype(jnp.bfloat16)
    attended = jnp.einsum(
        "qk,kd->qd", rounded, value_head, preferred_element_type=jnp.float32
    ).astype(jnp.bfloat16)
    weight_grads = jnp.einsum(
        "qd,kd->qk", grad_head, value_head, preferred_element_type=jnp.float32
    )
    centre = jnp.sum(weights * weight_grads, axis=-1, keepdims=True)
    score_grads = (weights * (weight_grads - centre)).astype(jnp.bfloat16)
    grad_query = (
        jnp.einsum("qk,kd->qd", score_grads, key_head, preferred_element_type=jnp.float32) * scaling
    ).astype(jnp.bfloat16)
    key_grads = (
        jnp.einsum("qk,qd->kd", score_grads, query_head, preferred_element_type=jnp.float32)
        * scaling
    )
    value_grads = jnp.einsum("qk,qd->kd", rounded, grad_head, preferred_element_type=jnp.float32)
    return (attended, grad_query, key_grads, value_grads)


def body(query_rows, key_rows, value_rows, grad_out):
    block_len, width_all = query_rows.shape
    head_count = width_all // HEAD_DIM
    seq_count = lax.axis_size("seq")
    grp_count = lax.axis_size(GRP)
    block_count = grp_count * seq_count
    rows_one = block_len // POOL1
    rows_two = rows_one // MERGE
    scaling = HEAD_DIM ** (-0.5)
    band = block_len + 2 * NEAR
    stacked = jnp.stack([key_rows, value_rows])
    extended = extended_2(stacked, ((GRP_SEQ, 1),), NEAR)
    pooled_one = pool_rows(stacked, POOL1).astype(jnp.bfloat16)
    group_one = gather_directly(pooled_one, "seq", 1)
    group_two = pool_rows(group_one, MERGE).astype(jnp.bfloat16)
    coarse_all = lax.all_gather(group_two, GRP, axis=1, tiled=True)
    index_all = lax.axis_index(GRP_SEQ)
    seq_place = lax.axis_index("seq")
    group_index = lax.axis_index(GRP)
    tokens = index_all * block_len + jnp.arange(band, dtype=jnp.int32) - NEAR
    band_live = (tokens >= 0) & (tokens < block_count * block_len)
    pool_block = jnp.arange(seq_count * rows_one, dtype=jnp.int32) // rows_one
    pool_live = jnp.abs(pool_block - seq_place) > 1
    coarse_group = jnp.arange(block_count * rows_two, dtype=jnp.int32) // (seq_count * rows_two)
    coarse_live = coarse_group != group_index
    bias_row = jnp.where(
        jnp.concatenate([band_live, pool_live, coarse_live]), 0.0, NEG_FILL
    ).astype(jnp.float32)
    key_set = jnp.concatenate([extended[0], group_one[0], coarse_all[0]], axis=0)
    value_set = jnp.concatenate([extended[1], group_one[1], coarse_all[1]], axis=0)
    operands = (
        split_heads(query_rows, head_count),
        split_heads(grad_out, head_count),
        split_heads(key_set, head_count),
        split_heads(value_set, head_count),
    )
    results = lax.map(lambda operand: head_pass(operand, bias_row, scaling), operands)
    attended = join_heads(results[0])
    grad_query = join_heads(results[1])
    set_grads = jnp.stack([join_heads(results[2]), join_heads(results[3])])
    band_grads = set_grads[:, :band]
    pool_grads = set_grads[:, band : band + seq_count * rows_one]
    coarse_grads = set_grads[:, band + seq_count * rows_one :]
    from_next = from_behind(band_grads[:, :NEAR], GRP_SEQ, -1)
    from_prev = from_behind(band_grads[:, NEAR + block_len :], GRP_SEQ, 1)
    own_rows = band_grads[:, NEAR : NEAR + block_len]
    own_rows = own_rows.at[:, block_len - NEAR :].add(from_next)
    own_rows = own_rows.at[:, :NEAR].add(from_prev)
    across = summed_rows(coarse_grads.astype(jnp.bfloat16), GRP, (1, 0), 1).astype(jnp.float32)
    pool_grads = pool_grads + expand_rows(across, MERGE) / MERGE
    own_one = lax.psum_scatter(
        pool_grads.astype(jnp.bfloat16), "seq", scatter_dimension=1, tiled=True
    ).astype(jnp.float32)
    totals = own_rows + expand_rows(own_one, POOL1) / POOL1
    return (attended, grad_query, totals[0].astype(jnp.bfloat16), totals[1].astype(jnp.bfloat16))


def solution(mesh):
    split = Mesh(mesh.devices.reshape(2, 8, mesh.shape["seq"]), ("grp_0", "grp_1", "seq"))
    placed = (P(GRP_SEQ, None), P(GRP_SEQ, None), P(GRP_SEQ, None), P(GRP_SEQ, None))
    return jax.shard_map(
        body,
        mesh=split,
        in_specs=placed,
        out_specs=(P(GRP_SEQ, None), P(GRP_SEQ, None), P(GRP_SEQ, None), P(GRP_SEQ, None)),
        check_vma=False,
    )
```

profile of v0, /device:TPU:1, one launch (start us, length us, event | category | flops | bytes accessed | tf_op | source)
XLA Modules:
  0.0 492.2 jit_solution(14772478334168728747)
XLA Ops:
  9.9 36.5 %all_to_all.5 = bf16[16,2,32,1024]{3,2,1,0:T(8,128)(2,1)S(1)} all-to-all(bf16[16,2,32,1024]{3,2,1,0:T(8,128)(2,1)S(1)} %broadcast_in_dim.41), channel_id=1, replica_groups=mesh['grp_0'=2,'grp_1'=8,'seq'=16] {'seq'}, dimensions={0} | all-to-all | bytes 4194304 | tf_op jit(solution)/shard_map/all_to_all | solution.py:46
  52.0 2.6 fusion.43
  56.6 3.6 collective-permute-start.1
  64.8 3.8 collective-permute-done
  68.6 4.7 collective-permute-done.1
  82.2 30.9 %all-gather.2.cloned.1.call-done = bf16[2,512,1024]{2,1,0:T(8,128)(2,1)} async-done(((bf16[2,32,1024]{2,1,0:T(8,128)(2,1)}), bf16[2,512,1024]{2,1,0:T(8,128)(2,1)}) %all-gather.2.cloned.1.call-update) | async-done | bytes 2097168 | tf_op jit(solution)/shard_map/all_gather | solution.py:143
  113.1 3.0 fusion.57
  120.6 5.5 %maximum_bitcast_fusion = (bf16[8,2048,128]{1,2,0:T(8,128)(2,1)}, bf16[8,2048,128]{1,2,0:T(8,128)(2,1)}) fusion(bf16[512,8,128]{0,2,1:T(8,128)(2,1)} %bitcast.162, bf16[512,8,128]{0,2,1:T(8,128)(2,1)} %copy.70, bf16[1024,8,128]{0,2,1:T(8,128)(2,1)} %bitcast.159, bf16[512,8,128]{0,2,1:T(8,128)(2,1)} %bitcast.161, bf16[512,8,128]{0,2,1:T(8,128)(2,1)S(1)} %copy.72, ...), kind=kLoop, calls=%fused_computation.49 | loop fusion | flops 25165824 | bytes 16777216 | tf_op jit(solution)/shard_map/transpose | solution.py:94
  126.1 145.9 %while.18 = (s32[]{:T(128)}, bf16[8,512,128]{2,1,0:T(8,128)(2,1)}, bf16[8,512,128]{2,1,0:T(8,128)(2,1)}, f32[8,2048,128]{2,1,0:T(8,128)}, f32[8,2048,128]{2,1,0:...) while((s32[]{:T(128)}, bf16[8,512,128]{2,1,0:T(8,128)(2,1)}, ...), condition=%wide.region_6.7_spmd, body=%wide.region_2.6_spmd.sunk | while | flops 1642527232 | bytes 44908660 | solution.py:164
  129.0 2.8 fusion.86
  138.5 3.3 fusion.89
  147.3 2.8 fusion.86
  156.7 3.2 fusion.89
  159.9 2.7 fusion.88
  165.5 2.8 fusion.86
  175.0 3.2 fusion.89
  178.2 2.6 fusion.88
  183.7 2.8 fusion.86
  193.2 3.2 fusion.89
  196.4 2.6 fusion.88
  201.9 2.8 fusion.86
  211.4 3.3 fusion.89
  220.2 2.8 fusion.86
  229.7 3.2 fusion.89
  232.9 2.7 fusion.88
  238.4 2.8 fusion.86
  247.9 3.2 fusion.89
  251.1 2.6 fusion.88
  256.7 2.8 fusion.86
  266.1 3.2 fusion.89
  269.3 2.7 fusion.88
  272.0 10.7 %copy.81 = f32[2048,8,128]{2,1,0:T(8,128)} copy(f32[2048,8,128]{2,0,1:T(8,128)} %bitcast.154) | data formatting | bytes 16777216 | tf_op jit(solution)/shard_map/transpose | solution.py:98
  282.7 9.2 %stack_reshape.7 = f32[1,2048,1024]{2,1,0:T(8,128)} reshape(f32[2048,8,128]{2,1,0:T(8,128)} %copy.81) | data formatting | bytes 16777216 | tf_op jit(solution)/shard_map/stack;reshape | solution.py:167
  291.9 10.7 %copy.80 = f32[2048,8,128]{2,1,0:T(8,128)} copy(f32[2048,8,128]{2,0,1:T(8,128)} %bitcast.155) | data formatting | bytes 16777216 | tf_op jit(solution)/shard_map/transpose | solution.py:98
  302.6 9.3 %stack_reshape.6 = f32[1,2048,1024]{2,1,0:T(8,128)} reshape(f32[2048,8,128]{2,1,0:T(8,128)} %copy.80) | data formatting | bytes 16777216 | tf_op jit(solution)/shard_map/stack;reshape | solution.py:167
  311.8 4.2 constant_dynamic-update-slice_fusion.1
  316.1 4.2 constant_dynamic-update-slice_fusion
  320.3 5.7 %copy-done = f32[2,2048,1024]{2,1,0:T(8,128)} copy-done((f32[2,2048,1024]{2,1,0:T(8,128)}, f32[2,2048,1024]{2,1,0:T(8,128)S(1)}, u32[]{:S(2)}) %copy-start) | copy-done | bytes 16777240
  328.0 44.1 %reduce-scatter.4.cloned.1.call-done = bf16[2,2,32,1024]{3,2,1,0:T(8,128)(2,1)} async-done(((bf16[16,2,32,1024]{3,2,1,0:T(8,128)(2,1)}), bf16[2,2,32,1024]{3,2,1,0:T(8,128)(2,1)}) %reduce-scatter.4.cloned.1.call-update) | async-done | bytes 262160 | tf_op jit(solution)/shard_map/reduce_scatter | solution.py:65
  372.2 22.1 %reduce-scatter.6.cloned.1.call-done = bf16[1,2,32,1024]{3,2,1,0:T(8,128)(2,1)} async-done(((bf16[2,2,32,1024]{3,2,1,0:T(8,128)(2,1)}), bf16[1,2,32,1024]{3,2,1,0:T(8,128)(2,1)}) %reduce-scatter.6.cloned.1.call-update) | async-done | bytes 131088 | tf_op jit(solution)/shard_map/reduce_scatter | solution.py:65
  395.1 7.4 %fusion.39 = (bf16[2,512,1024]{2,1,0:T(8,128)(2,1)}, f32[2,512,1024]{2,1,0:T(8,128)}) fusion(f32[2,2048,1024]{2,1,0:T(8,128)} %copy-done, f32[2,32,1024]{2,1,0:T(8,128)S(1)} %multiply_bitcast_fusion), kind=kLoop, calls=%fused_computation.47 | loop fusion | flops 2097152 | bytes 14942208 | tf_op jit(solution)/shard_map/convert_element_type | solution.py:179
  402.6 2.7 fusion.54
  407.8 3.0 collective-permute-start.3
  413.1 19.5 %collective-permute-done.2 = f32[2,256,1024]{2,1,0:T(8,128)S(1)} collective-permute-done((f32[2,256,1024]{2,1,0:T(8,128)S(1)}, f32[2,256,1024]{2,1,0:T(8,128)S(1)}, u32[]{:S(2)}, u32[]{:S(2)}) %collective-permute-start.2) | collective-permute-done | bytes 2097184 | tf_op jit(solution)/shard_map/ppermute | solution.py:56
  432.6 3.3 fusion.42
  435.9 3.3 fusion.41
  439.2 41.2 %reduce-scatter.8.cloned.1.call-done = bf16[2,32,1024]{2,1,0:T(8,128)(2,1)} async-done(((bf16[2,512,1024]{2,1,0:T(8,128)(2,1)}), bf16[2,32,1024]{2,1,0:T(8,128)(2,1)}) %reduce-scatter.8.cloned.1.call-update) | async-done | bytes 131088 | tf_op jit(solution)/shard_map/reduce_scatter | solution.py:178
  481.3 2.9 fusion.40
  (95 shorter events, 119.7 us)
Async XLA Ops:
  7.2 105.9 %all-gather.2.cloned.1.call-start = ((), (), s32[]{:S(2)}) async-start(), calls=%async_computation.4 | async-start | bytes 2228224 | tf_op jit(solution)/shard_map/all_gather | solution.py:143
  48.2 323.9 %reduce-scatter.4.cloned.1.call-start = ((), (), s32[]{:S(2)}) async-start(), calls=%async_computation.5 | async-start | bytes 2359296 | tf_op jit(solution)/shard_map/reduce_scatter | solution.py:65
  54.7 14.0 %collective-permute-start = (bf16[2,256,1024]{1,2,0:T(8,128)(2,1)}, bf16[2,256,1024]{1,2,0:T(8,128)(2,1)}, u32[]{:S(2)}, u32[]{:S(2)}) collective-permute-start(bf16[2,256,1024]{1,2,0:T(8,128)(2,1)} %get-tuple-element.163), channel_id=1, source_target_pairs={{0,1},{1,2},{2,3},{3,4},{4,5},{5,6},{6,7},{7,8},{8,9},{9,10},{10,1... | collective-permute-start | bytes 3145736 | tf_op jit(solution)/shard_map/ppermute | solution.py:26
  56.6 16.7 %collective-permute-start.1 = (bf16[2,256,1024]{1,2,0:T(8,128)(2,1)}, bf16[2,256,1024]{1,2,0:T(8,128)(2,1)}, u32[]{:S(2)}, u32[]{:S(2)}) collective-permute-start(bf16[2,256,1024]{1,2,0:T(8,128)(2,1)} %get-tuple-element.164), channel_id=1, source_target_pairs={{1,0},{2,1},{3,2},{4,3},{5,4},{6,5},{7,6},{8,7},{9,8},{10,9},{11,1... | collective-permute-start | bytes 3145736 | tf_op jit(solution)/shard_map/ppermute | solution.py:27
  79.1 1.2 copy-start.2
  82.1 38.5 %copy-start.1 = (bf16[1,1024,1024]{1,2,0:T(8,128)(2,1)S(1)}, bf16[1,1024,1024]{1,2,0:T(8,128)(2,1)}, u32[]{:S(2)}) copy-start(bf16[1,1024,1024]{1,2,0:T(8,128)(2,1)} %get-tuple-element.155) | copy-start | bytes 6291460
  320.3 5.7 %copy-start = (f32[2,2048,1024]{2,1,0:T(8,128)}, f32[2,2048,1024]{2,1,0:T(8,128)S(1)}, u32[]{:S(2)}) copy-start(f32[2,2048,1024]{2,1,0:T(8,128)S(1)} %constant_dynamic-update-slice_fusion) | copy-start | bytes 50331652
  328.0 66.3 %reduce-scatter.6.cloned.1.call-start = ((), (), s32[]{:S(2)}) async-start(), calls=%async_computation.6 | async-start | bytes 393216 | tf_op jit(solution)/shard_map/reduce_scatter | solution.py:65
  372.1 108.3 %reduce-scatter.8.cloned.1.call-start = ((), (), s32[]{:S(2)}) async-start(), calls=%async_computation.7 | async-start | bytes 2228224 | tf_op jit(solution)/shard_map/reduce_scatter | solution.py:178
  402.5 8.3 %copy-start.4 = (bf16[8,512,128]{2,1,0:T(8,128)(2,1)S(1)}, bf16[8,512,128]{2,1,0:T(8,128)(2,1)}, u32[]{:S(2)}) copy-start(bf16[8,512,128]{2,1,0:T(8,128)(2,1)} %get-tuple-element.83) | copy-start | bytes 3145732
  402.6 9.4 %copy-start.3 = (bf16[8,512,128]{2,1,0:T(8,128)(2,1)S(1)}, bf16[8,512,128]{2,1,0:T(8,128)(2,1)}, u32[]{:S(2)}) copy-start(bf16[8,512,128]{2,1,0:T(8,128)(2,1)} %get-tuple-element.84) | copy-start | bytes 3145732
  405.3 27.4 %collective-permute-start.2 = (f32[2,256,1024]{2,1,0:T(8,128)S(1)}, f32[2,256,1024]{2,1,0:T(8,128)S(1)}, u32[]{:S(2)}, u32[]{:S(2)}) collective-permute-start(f32[2,256,1024]{2,1,0:T(8,128)S(1)} %get-tuple-element.154), channel_id=1, source_target_pairs={{1,0},{2,1},{3,2},{4,3},{5,4},{6,5},{7,6},{8,7},{9,8},{10,9},{11,1... | collective-permute-start | bytes 6291464 | tf_op jit(solution)/shard_map/ppermute | solution.py:56
  407.8 28.1 %collective-permute-start.3 = (f32[2,256,1024]{2,1,0:T(8,128)S(1)}, f32[2,256,1024]{2,1,0:T(8,128)S(1)}, u32[]{:S(2)}, u32[]{:S(2)}) collective-permute-start(f32[2,256,1024]{2,1,0:T(8,128)S(1)} %get-tuple-element.153), channel_id=1, source_target_pairs={{0,1},{1,2},{2,3},{3,4},{4,5},{5,6},{6,7},{7,8},{8,9},{9,10},{10,1... | collective-permute-start | bytes 6291464 | tf_op jit(solution)/shard_map/ppermute | solution.py:56
Sparse Core Ops, SparseCore 0:
  48.3 64.7 all-gather.1
  328.1 43.9 reduce-scatter.3
  374.6 19.5 reduce-scatter.5
  402.7 77.6 reduce-scatter.7
where the time goes:
time: 495 us; the launch traced here: 492 us
  waiting for transfers between devices  166 us (34%)
  matrix products  126 us (25%)
  local copies, waits for them, and re-layouts  85.3 us (17%)
  other arithmetic  53.1 us (11%)
  blocking collectives  36.5 us (7%)
  between operations  14 us (3%)
  starting transfers between devices  11.2 us (2%)
    reduce_scatter x2, waiting for transfers between devices, own_block(): parts = lax.psum_scatter(parts, axes[k], scatter_dimension=0, tiled=True)  66.1 us
    reduce_scatter x1, waiting for transfers between devices, body(): lax.psum_scatter(pool_grads.astype(jnp.bfloat16), 'seq', scatter_dimensio...  41.2 us
    all_to_all x1, blocking collectives, from_everyone(): return lax.all_to_all(copies, axis, split_axis=0, concat_axis=0, tiled=True)  36.5 us
    all_gather x1, waiting for transfers between devices, body(): coarse_all = lax.all_gather(group_two, GRP, axis=1, tiled=True)  30.9 us
    dot_general x8, matrix products, head_pass(): jnp.einsum('qk,qd->kd', rounded, grad_head, preferred_element_type=jnp.fl...  25.9 us
    another operation x3, local copies, waits for them, and re-layouts, body(): set_grads = jnp.stack([join_heads(results[2]), join_heads(results[3])])  22.8 us
    dot_general x8, matrix products, head_pass(): jnp.einsum('qk,kd->qd', rounded, value_head, preferred_element_type=jnp.f...  22.7 us
    transpose x2, local copies, waits for them, and re-layouts, join_heads(): stacked.transpose(1, 0, 2)  21.3 us
  transfers between devices with their start and end apart: 8, of which 7 were waited for; matrix products, arithmetic and copies ran while one was open for 6% of the time, Pallas kernels for 0%

commit v1 on v0

v1 whole, which is shorter than its diff:
```python
import functools

import jax
import jax.numpy as jnp
from jax import lax
from jax.experimental import pallas as pl
from jax.experimental.pallas import tpu as pltpu
from jax.sharding import PartitionSpec as P

F32 = jnp.float32
BF16 = jnp.bfloat16
HEADS = 8
DIM = 128
BLOCK = 512
NEAR = 256
POOL = 16
ONE = BLOCK // POOL
TWO = ONE // POOL
PLACES = 16
GROUPS = 16
SET = 2048
OWN, PREV, NEXT, LEVEL1, LEVEL2 = 0, 512, 768, 1024, 1536
SCALE = DIM**-0.5
SCALE2 = SCALE * 1.4426950408889634
FILL = -1e30
MESH = pl.DeviceIdType.MESH
CHUNKS = 4
PER = HEADS // CHUNKS
STEP = 512

IN_KV, IN_QG, POOLED, FROM_PREV, FROM_NEXT, COARSE, PAIR_ONE, PAIR_TWO = range(8)
GRAD_PREV, GRAD_NEXT, PAIR_GRAD, COARSE_GRAD, POOL_GRAD, OUT_Q, OUT_KV = range(8, 15)
STAGES = 15


def dot_nt(a, b):
    return lax.dot_general(a, b, (((1,), (1,)), ((), ())), preferred_element_type=F32)


def dot_tn(a, b):
    return lax.dot_general(a, b, (((0,), (0,)), ((), ())), preferred_element_type=F32)


def dot_nn(a, b):
    return jnp.dot(a, b, preferred_element_type=F32)


def attend(h, q_all, g_all, kv, bias, att, gq, gown, gset, score, dprob, total):
    query, grad = q_all[h], g_all[h]
    parts = [pl.ds(i * STEP, STEP) for i in range(SET // STEP)]

    def folded(x, op):
        return op(x.reshape(STEP // 8, 8, BLOCK), axis=0)

    top = None
    for rows in parts:
        s = dot_nt(kv[h, 0, rows, :], query)
        b = bias[rows, :]
        s = s + jnp.concatenate([b] * (BLOCK // DIM), axis=1)
        score[rows, :] = s
        part = folded(s, jnp.max)
        top = part if top is None else jnp.maximum(top, part)
    top = jnp.max(top, axis=0, keepdims=True)
    norm = mixed = None
    for rows in parts:
        dp = dot_nt(kv[h, 1, rows, :], grad)
        e = jnp.exp2((score[rows, :] - top) * SCALE2)
        score[rows, :] = e
        dprob[rows, :] = dp
        part, other = folded(e, jnp.sum), folded(e * dp, jnp.sum)
        norm = part if norm is None else norm + part
        mixed = other if mixed is None else mixed + other
    inverse = 1.0 / jnp.sum(norm, axis=0, keepdims=True)
    delta = jnp.sum(mixed, axis=0, keepdims=True) * inverse
    for i, rows in enumerate(parts):
        p = score[rows, :] * inverse
        pb = p.astype(BF16)
        ds = (p * (dprob[rows, :] - delta)).astype(BF16)
        out, dq = dot_tn(kv[h, 1, rows, :], pb), dot_tn(kv[h, 0, rows, :], ds)
        if i == 0:
            total[0], total[1] = out, dq
        else:
            total[0] += out
            total[1] += dq
        dv, dk = dot_nn(pb, grad), dot_nn(ds, query) * SCALE
        if i * STEP < BLOCK:
            gown[h, 0, rows, :] = dk
            gown[h, 1, rows, :] = dv
        else:
            there = pl.ds(i * STEP - BLOCK, STEP)
            gset[h, 0, there, :] = dk.astype(BF16)
            gset[h, 1, there, :] = dv.astype(BF16)
    att[h] = total[0].T.astype(BF16)
    gq[h] = (total[1].T * SCALE).astype(BF16)


def kernel(
    q_hbm, k_hbm, v_hbm, g_hbm, att_hbm, gq_hbm, gk_hbm, gv_hbm,
    kv, q_all, g_all, pooled, gown, gset, pair, csend, crecv, psend, precv, hrecv,
    bias, mean, spread, score, dprob, total, att, gq, final, send, recv,
):
    g, s = lax.axis_index("grp"), lax.axis_index("seq")
    core = lax.rem(s, 2)
    other = 1 - core
    sibling = (g, s + 1 - 2 * core)
    has_prev = (g + s) > 0
    has_next = (g + s) < GROUPS + PLACES - 2
    up_group = lax.rem(g + lax.div(s + 1, PLACES), GROUPS)
    after = (up_group, lax.rem(s + 1, PLACES))
    low_group = lax.rem(g + GROUPS - 1 + lax.div(s + PLACES - 1, PLACES), GROUPS)
    before = (low_group, lax.rem(s + PLACES - 1, PLACES))
    mine_one = pl.multiple_of(s * ONE, ONE)
    mine_two = pl.multiple_of(g * ONE, ONE)

    def heads(ch):
        return pl.ds(ch * PER, PER)

    def lanes(h):
        return pl.ds(pl.multiple_of(h * DIM, DIM), DIM)

    def push(stage, ch, src, dst, device):
        pltpu.make_async_remote_copy(
            src_ref=src, dst_ref=dst, send_sem=send.at[stage, ch], recv_sem=recv.at[stage, ch],
            device_id=device, device_id_type=MESH,
        ).start()

    def await_bytes(sems, stage, ch, ref):
        pltpu.make_async_copy(ref, ref, sems.at[stage, ch]).wait()

    def each_head(ch, do):
        lax.fori_loop(0, PER, lambda i, _: (do(ch * PER + i), 0)[1], 0)

    def each_peer(do):
        lax.fori_loop(1, PLACES, lambda j, _: (do(j), 0)[1], 0)

    def fetch(h, _):
        ch = lax.div(h, PER)
        for plane, src in enumerate((k_hbm, v_hbm)):
            pltpu.make_async_copy(
                src.at[:, lanes(h)], kv.at[h, plane, pl.ds(OWN, BLOCK), :], recv.at[IN_KV, ch]
            ).start()
        for dst, src in ((q_all, q_hbm), (g_all, g_hbm)):
            pltpu.make_async_copy(src.at[:, lanes(h)], dst.at[h], recv.at[IN_QG, ch]).start()
        return 0

    lax.fori_loop(0, HEADS, fetch, 0)

    barrier = pltpu.get_barrier_semaphore()

    def greet(j):
        for device in ((g, lax.rem(s + j, PLACES)), (lax.rem(g + j, GROUPS), s)):
            pl.semaphore_signal(barrier, inc=1, device_id=device, device_id_type=MESH)

    each_peer(greet)
    crosses_up = jnp.logical_and(s == PLACES - 1, has_next)
    crosses_down = jnp.logical_and(s == 0, has_prev)

    @pl.when(crosses_up)
    def _():
        pl.semaphore_signal(barrier, inc=1, device_id=after, device_id_type=MESH)

    @pl.when(crosses_down)
    def _():
        pl.semaphore_signal(barrier, inc=1, device_id=before, device_id_type=MESH)

    row = lax.broadcasted_iota(jnp.int32, (SET, DIM), 0)
    one = lax.shift_right_logical(row - LEVEL1, 5)
    two = lax.shift_right_logical(row - LEVEL2, 5)
    dead_one = (row >= LEVEL1) & (row < LEVEL2) & (one >= s - 1) & (one <= s + 1)
    dead_two = (row >= LEVEL2) & (two == g)
    no_prev = (row >= PREV) & (row < NEXT) & (g + s == 0)
    no_next = (row >= NEXT) & (row < LEVEL1) & (g + s == GROUPS + PLACES - 2)
    bias[...] = jnp.where(dead_one | dead_two | no_prev | no_next, FILL, 0.0)
    wide = (lax.broadcasted_iota(jnp.int32, (ONE, BLOCK), 0), lax.broadcasted_iota(jnp.int32, (ONE, BLOCK), 1))
    mean[...] = jnp.where(lax.shift_right_logical(wide[1], 4) == wide[0], 1.0 / POOL, 0.0).astype(BF16)
    tall = (lax.broadcasted_iota(jnp.int32, (BLOCK, ONE), 0), lax.broadcasted_iota(jnp.int32, (BLOCK, ONE), 1))
    spread[...] = jnp.where(lax.shift_right_logical(tall[0], 4) == tall[1], 1.0 / POOL, 0.0).astype(BF16)

    @pl.when(jnp.logical_not(has_prev))
    def _():
        kv[:, :, PREV:NEXT, :] = jnp.zeros((HEADS, 2, NEAR, DIM), BF16)
        hrecv[:, 0] = jnp.zeros((HEADS, 2, NEAR, DIM), BF16)

    @pl.when(jnp.logical_not(has_next))
    def _():
        kv[:, :, NEXT:LEVEL1, :] = jnp.zeros((HEADS, 2, NEAR, DIM), BF16)
        hrecv[:, 1] = jnp.zeros((HEADS, 2, NEAR, DIM), BF16)

    crosses = jnp.logical_or(crosses_up, crosses_down)

    @pl.when(crosses)
    def _():
        pl.semaphore_wait(barrier, PLACES + GROUPS - 1)

    @pl.when(jnp.logical_not(crosses))
    def _():
        pl.semaphore_wait(barrier, PLACES + GROUPS - 2)

    def spread_rows(x):
        high = x.astype(BF16)
        low = (x - high.astype(F32)).astype(BF16)
        return dot_nn(spread[...], high) + dot_nn(spread[...], low)

    def send_pooled(ch):
        hs = heads(ch)
        await_bytes(recv, IN_KV, ch, kv.at[hs, :, pl.ds(OWN, BLOCK), :])

        def pool(h):
            for plane in range(2):
                pooled[h, plane] = dot_nn(mean[...], kv[h, plane, pl.ds(OWN, BLOCK), :]).astype(BF16)
            kv[h, core, pl.ds(LEVEL1 + mine_one, ONE), :] = pooled[h, core]

        each_head(ch, pool)

        def to(j):
            there = lax.rem(s + j, PLACES)
            plane = lax.rem(there, 2)
            push(
                POOLED, ch, pooled.at[hs, plane],
                kv.at[hs, plane, pl.ds(LEVEL1 + mine_one, ONE), :], (g, there),
            )

        each_peer(to)

        @pl.when(has_next)
        def _():
            push(FROM_PREV, ch, kv.at[hs, :, pl.ds(OWN + BLOCK - NEAR, NEAR), :], kv.at[hs, :, pl.ds(PREV, NEAR), :], after)

        @pl.when(has_prev)
        def _():
            push(FROM_NEXT, ch, kv.at[hs, :, pl.ds(OWN, NEAR), :], kv.at[hs, :, pl.ds(NEXT, NEAR), :], before)

    def all_but_one(ref, ch):
        return ref.at[heads(ch), pl.ds(0, BLOCK - ONE), :]

    def send_coarse(ch):
        hs = heads(ch)
        await_bytes(recv, POOLED, ch, kv.at[hs, core, pl.ds(LEVEL1, BLOCK - ONE), :])
        whole = kv.at[hs, core, pl.ds(LEVEL1, BLOCK), :]
        push(PAIR_ONE, ch, whole, whole, sibling)

        def pool(h):
            kv[h, core, pl.ds(LEVEL2 + mine_two, ONE), :] = dot_nn(
                mean[...], kv[h, core, pl.ds(LEVEL1, BLOCK), :]
            ).astype(BF16)

        each_head(ch, pool)
        own = kv.at[hs, core, pl.ds(LEVEL2 + mine_two, ONE), :]
        each_peer(lambda j: push(COARSE, ch, own, own, (lax.rem(g + j, GROUPS), s)))

    def pass_coarse(ch):
        hs = heads(ch)
        await_bytes(recv, COARSE, ch, kv.at[hs, core, pl.ds(LEVEL2, BLOCK - ONE), :])
        whole = kv.at[hs, core, pl.ds(LEVEL2, BLOCK), :]
        push(PAIR_TWO, ch, whole, whole, sibling)

    def compute(ch):
        hs = heads(ch)
        await_bytes(recv, IN_QG, ch, kv.at[hs, :, pl.ds(OWN, BLOCK), :])
        await_bytes(recv, PAIR_ONE, ch, kv.at[hs, other, pl.ds(LEVEL1, BLOCK), :])
        await_bytes(recv, PAIR_TWO, ch, kv.at[hs, other, pl.ds(LEVEL2, BLOCK), :])

        @pl.when(has_prev)
        def _():
            await_bytes(recv, FROM_PREV, ch, kv.at[hs, :, pl.ds(PREV, NEAR), :])

        @pl.when(has_next)
        def _():
            await_bytes(recv, FROM_NEXT, ch, kv.at[hs, :, pl.ds(NEXT, NEAR), :])

        each_head(
            ch,
            lambda h: attend(h, q_all, g_all, kv, bias, att, gq, gown, gset, score, dprob, total),
        )
        push(PAIR_GRAD, ch, gset.at[hs, other, pl.ds(LEVEL1 - BLOCK, 2 * BLOCK), :], pair.at[hs], sibling)

        @pl.when(has_prev)
        def _():
            push(GRAD_NEXT, ch, gset.at[hs, :, pl.ds(PREV - BLOCK, NEAR), :], hrecv.at[hs, 1], before)

        @pl.when(has_next)
        def _():
            push(GRAD_PREV, ch, gset.at[hs, :, pl.ds(NEXT - BLOCK, NEAR), :], hrecv.at[hs, 0], after)

        def store(h):
            for src, dst in ((att, att_hbm), (gq, gq_hbm)):
                pltpu.make_async_copy(src.at[h], dst.at[:, lanes(h)], send.at[OUT_Q, ch]).start()

        each_head(ch, store)

    def send_coarse_grads(ch):
        hs = heads(ch)
        await_bytes(recv, PAIR_GRAD, ch, pair.at[hs])

        def add(h):
            mine = gset[h, core, pl.ds(LEVEL2 - BLOCK, BLOCK), :].astype(F32)
            csend[h] = (mine + pair[h, pl.ds(BLOCK, BLOCK), :].astype(F32)).astype(BF16)
            crecv[h, pl.ds(mine_two, ONE), :] = csend[h, pl.ds(mine_two, ONE), :]

        each_head(ch, add)

        def to(j):
            there = lax.rem(g + j, GROUPS)
            rows = pl.ds(pl.multiple_of(there * ONE, ONE), ONE)
            push(COARSE_GRAD, ch, csend.at[hs, rows, :], crecv.at[hs, pl.ds(mine_two, ONE), :], (there, s))

        each_peer(to)

    def send_pool_grads(ch):
        hs = heads(ch)
        await_bytes(recv, COARSE_GRAD, ch, all_but_one(crecv, ch))

        def add(h):
            coarse = crecv[h, pl.ds(0, ONE), :].astype(F32)
            for i in range(1, GROUPS):
                coarse = coarse + crecv[h, pl.ds(i * ONE, ONE), :].astype(F32)
            mine = gset[h, core, pl.ds(LEVEL1 - BLOCK, BLOCK), :].astype(F32)
            both = mine + pair[h, pl.ds(0, BLOCK), :].astype(F32)
            psend[h] = (both + spread_rows(coarse)).astype(BF16)
            precv[h, pl.ds(mine_one, ONE), :] = psend[h, pl.ds(mine_one, ONE), :]

        each_head(ch, add)

        def to(j):
            there = lax.rem(s + j, PLACES)
            rows = pl.ds(pl.multiple_of(there * ONE, ONE), ONE)
            push(POOL_GRAD, ch, psend.at[hs, rows, :], precv.at[hs, pl.ds(mine_one, ONE), :], (g, there))

        each_peer(to)

    def finish(ch):
        hs = heads(ch)
        await_bytes(recv, POOL_GRAD, ch, all_but_one(precv, ch))

        @pl.when(has_prev)
        def _():
            await_bytes(recv, GRAD_PREV, ch, hrecv.at[hs, 0])

        @pl.when(has_next)
        def _():
            await_bytes(recv, GRAD_NEXT, ch, hrecv.at[hs, 1])

        def add(h):
            for plane, dst in enumerate((gk_hbm, gv_hbm)):
                level = precv[h, pl.ds(plane * ONE, ONE), :].astype(F32)
                for i in range(1, PLACES // 2):
                    level = level + precv[h, pl.ds((2 * i + plane) * ONE, ONE), :].astype(F32)
                sums = gown[h, plane] + spread_rows(level)
                for side in range(2):
                    rows = slice(side * NEAR, (side + 1) * NEAR)
                    final[h, plane, pl.ds(side * NEAR, NEAR), :] = (
                        sums[rows] + hrecv[h, side, plane].astype(F32)
                    ).astype(BF16)
                pltpu.make_async_copy(final.at[h, plane], dst.at[:, lanes(h)], send.at[OUT_KV, ch]).start()

        each_head(ch, add)

    stages = (send_pooled, send_coarse, pass_coarse, compute, send_coarse_grads, send_pool_grads, finish)

    def step(t, _):
        for lag, stage in enumerate(stages):
            pl.when(jnp.logical_and(t >= lag, t < CHUNKS + lag))(functools.partial(stage, t - lag))
        return 0

    lax.fori_loop(0, CHUNKS + len(stages) - 1, step, 0)

    def drain(ch, _):
        hs = heads(ch)
        for stage, ref in (
            (POOLED, all_but_one(psend, ch)),
            (COARSE, all_but_one(psend, ch)),
            (PAIR_ONE, psend.at[hs]),
            (PAIR_TWO, psend.at[hs]),
            (PAIR_GRAD, pair.at[hs]),
            (COARSE_GRAD, all_but_one(csend, ch)),
            (POOL_GRAD, all_but_one(psend, ch)),
            (OUT_Q, pair.at[hs]),
            (OUT_KV, final.at[hs]),
        ):
            await_bytes(send, stage, ch, ref)

        @pl.when(has_prev)
        def _():
            await_bytes(send, FROM_NEXT, ch, hrecv.at[hs, 0])
            await_bytes(send, GRAD_NEXT, ch, hrecv.at[hs, 0])

        @pl.when(has_next)
        def _():
            await_bytes(send, FROM_PREV, ch, hrecv.at[hs, 0])
            await_bytes(send, GRAD_PREV, ch, hrecv.at[hs, 0])

        return 0

    lax.fori_loop(0, CHUNKS, drain, 0)


def body(query_rows, key_rows, value_rows, grad_out):
    shape = jax.ShapeDtypeStruct(query_rows.shape, BF16)
    rows = (HEADS, BLOCK, DIM)
    scratch = [
        ((HEADS, 2, SET, DIM), BF16),
        (rows, BF16),
        (rows, BF16),
        ((HEADS, 2, ONE, DIM), BF16),
        ((HEADS, 2, BLOCK, DIM), F32),
        ((HEADS, 2, SET - BLOCK, DIM), BF16),
        ((HEADS, 2 * BLOCK, DIM), BF16),
        (rows, BF16),
        (rows, BF16),
        (rows, BF16),
        (rows, BF16),
        ((HEADS, 2, 2, NEAR, DIM), BF16),
        ((SET, DIM), F32),
        ((ONE, BLOCK), BF16),
        ((BLOCK, ONE), BF16),
        ((SET, BLOCK), F32),
        ((SET, BLOCK), F32),
        ((2, DIM, BLOCK), F32),
        (rows, BF16),
        (rows, BF16),
        ((HEADS, 2, BLOCK, DIM), BF16),
    ]
    anywhere = pl.BlockSpec(memory_space=pl.ANY)
    return pl.pallas_call(
        kernel,
        out_shape=[shape] * 4,
        in_specs=[anywhere] * 4,
        out_specs=[anywhere] * 4,
        scratch_shapes=[pltpu.VMEM(*one) for one in scratch]
        + [pltpu.SemaphoreType.DMA((STAGES, CHUNKS))] * 2,
        compiler_params=pltpu.CompilerParams(
            collective_id=0, has_side_effects=True, vmem_limit_bytes=58 << 20
        ),
        name="hierarchical",
    )(query_rows, key_rows, value_rows, grad_out)


def solution(mesh):
    placed = P(("grp", "seq"), None)
    return jax.shard_map(
        body, mesh=mesh, in_specs=(placed,) * 4, out_specs=(placed,) * 4, check_vma=False
    )
```

time: 495 us -> 114 us (0.23)
  waiting for transfers between devices: 166 us -> 0 us
  matrix products: 126 us -> 0 us
  Pallas kernels: 0 us -> 106 us
  local copies, waits for them, and re-layouts: 85.3 us -> 6.53 us
  other arithmetic: 53.1 us -> 0 us
  blocking collectives: 36.5 us -> 0 us
  between operations: 14 us -> 0.65 us
  starting transfers between devices: 11.2 us -> 0 us
    dot_general x48 -> x0, matrix products: 126 us -> none  [the longest x8 25.9 us: head_pass(): jnp.einsum('qk,qd->kd', rounded, grad_head, preferred_element_type=jnp.fl...]
    reduce_scatter x3 -> x0, waiting for transfers between devices: 107 us -> none  [the longest x2 66.1 us: own_block(): parts = lax.psum_scatter(parts, axes[k], scatter_dimension=0, tiled=True)]
    pallas_call x0 -> x1, Pallas kernels: none -> 106 us  [body(): pl.pallas_call(kernel, out_shape=[shape] * 4, in_specs=[anywhere] * 4, ou...]
    all_to_all x1 -> x0, blocking collectives: 36.5 us -> none  [from_everyone(): return lax.all_to_all(copies, axis, split_axis=0, concat_axis=0, tiled=True)]
    all_gather x1 -> x0, waiting for transfers between devices: 30.9 us -> none  [body(): coarse_all = lax.all_gather(group_two, GRP, axis=1, tiled=True)]
    ppermute x4 -> x0, waiting for transfers between devices: 28 us -> none  [the longest x2 19.5 us: from_behind(): return lax.ppermute(block, axis, route)]
    transpose x3 -> x0, local copies, waits for them, and re-layouts: 22.9 us -> none  [the longest x2 21.3 us: join_heads(): stacked.transpose(1, 0, 2)]
    another operation x3 -> x0, local copies, waits for them, and re-layouts: 22.8 us -> none  [body(): set_grads = jnp.stack([join_heads(results[2]), join_heads(results[3])])]
  transfers between devices with their start and end apart: 8 -> 0, of which waited for: 7 -> 0; matrix products, arithmetic and copies ran while one was open for 6% -> 0% of each run, Pallas kernels for 0% -> 0%
where the time goes in v1:
time: 114 us
  Pallas kernels  106 us (93%)
  local copies, waits for them, and re-layouts  6.53 us (6%)
    pallas_call x1, Pallas kernels, body(): pl.pallas_call(kernel, out_shape=[shape] * 4, in_specs=[anywhere] * 4, ou...  106 us
    unnamed x10, local copies, waits for them, and re-layouts  6.53 us

profile of v1, /device:TPU:1, one launch (start us, length us, event | category | flops | bytes accessed | tf_op | source)
XLA Modules:
  0.0 113.6 jit_solution(15890767311788253296)
XLA Ops:
  0.6 106.4 %hierarchical.1 = (bf16[512,1024]{1,0:T(8,128)(2,1)}, bf16[512,1024]{1,0:T(8,128)(2,1)}, bf16[512,1024]{1,0:T(8,128)(2,1)}, bf16[512,1024]{1,0:T(8,128)(2,1)}) custom-call(bf16[512,1024]{1,0:T(8,128)(2,1)} %q_hbm.1, bf16[512,1024]{1,0:T(8,128)(2,1)} %k_hbm.1, bf16[512,1024]{1,0:T(8,128)(2,1)} %v_hbm.1, bf16[512,1024]{1,0:T(8,128)(2,1)} %g_hbm.1), custom_call_target="tpu_custom_call" | custom-call | tf_op jit(solution)/shard_map/hierarchical/pallas_call | solution.py:424
  107.1 0.0 copy-start.2
  107.1 2.4 %copy.12 = bf16[512,1024]{1,0:T(8,128)(2,1)} copy(bf16[512,1024]{1,0:T(8,128)(2,1)} %get-tuple-element.8) | data formatting | bytes 2097152
  109.4 0.0 copy-done.2
  109.5 0.0 copy-start.1
  109.5 1.0 copy.13
  110.4 0.6 copy-done.1
  111.1 0.0 copy-start
  111.1 1.0 copy.14
  112.0 0.6 copy-done
  112.7 1.0 copy.15
Async XLA Ops:
  107.1 2.4 %copy-start.2 = (bf16[512,1024]{1,0:T(8,128)(2,1)S(1)}, bf16[512,1024]{1,0:T(8,128)(2,1)}, u32[]{:S(2)}) copy-start(bf16[512,1024]{1,0:T(8,128)(2,1)} %get-tuple-element.9) | copy-start | bytes 3145732
  109.5 1.6 %copy-start.1 = (bf16[512,1024]{1,0:T(8,128)(2,1)S(1)}, bf16[512,1024]{1,0:T(8,128)(2,1)}, u32[]{:S(2)}) copy-start(bf16[512,1024]{1,0:T(8,128)(2,1)} %get-tuple-element.10) | copy-start | bytes 3145732
  111.1 1.6 %copy-start = (bf16[512,1024]{1,0:T(8,128)(2,1)S(1)}, bf16[512,1024]{1,0:T(8,128)(2,1)}, u32[]{:S(2)}) copy-start(bf16[512,1024]{1,0:T(8,128)(2,1)} %get-tuple-element.11) | copy-start | bytes 3145732

commit v2 on v1

v2 whole, which is shorter than its diff:
```python
import functools

import jax
import jax.numpy as jnp
from jax import lax
from jax.experimental import pallas as pl
from jax.experimental.pallas import tpu as pltpu
from jax.sharding import PartitionSpec as P

F32 = jnp.float32
BF16 = jnp.bfloat16
HEADS = 8
DIM = 128
BLOCK = 512
NEAR = 256
POOL = 16
ONE = BLOCK // POOL
TWO = ONE // POOL
PLACES = 16
GROUPS = 16
SET = 2048
OWN, PREV, NEXT, LEVEL1, LEVEL2 = 0, 512, 768, 1024, 1536
SCALE = DIM**-0.5
SCALE2 = SCALE * 1.4426950408889634
FILL = -1e30
MESH = pl.DeviceIdType.MESH
CHUNKS = 8
PER = HEADS // CHUNKS
STEP = 512

IN_KV, IN_QG, PAIR_POOL, ACROSS_HI, RIGHT, LEFT = range(0, 6)
FAR_RIGHT, FAR_LEFT, ACROSS_LO, UP1, DOWN1, UP2 = range(6, 12)
DOWN2, UP3, DOWN3, UP4, DOWN4, PAIR_SET = range(12, 18)
FROM_PREV, FROM_NEXT, PAIR_GRAD, GRAD_PREV, GRAD_NEXT, C_DOWN3 = range(18, 24)
C_UP3, C_DOWN4, C_UP4, C_DOWN1, C_UP1, C_DOWN2 = range(24, 30)
C_UP2, C_LO, R_FAR_LEFT, R_FAR_RIGHT, R_LEFT, R_RIGHT = range(30, 36)
R_HI, R_PAIR = range(36, 38)
TRANSFERS = 38


def dot_nt(a, b):
    return lax.dot_general(a, b, (((1,), (1,)), ((), ())), preferred_element_type=F32)


def dot_tn(a, b):
    return lax.dot_general(a, b, (((0,), (0,)), ((), ())), preferred_element_type=F32)


def dot_nn(a, b):
    return jnp.dot(a, b, preferred_element_type=F32)


def attend(h, q_all, g_all, kv, bias, att, gq, gown, gset, score, dprob, total):
    query, grad = q_all[h], g_all[h]
    parts = [pl.ds(i * STEP, STEP) for i in range(SET // STEP)]

    def folded(x, op):
        return op(x.reshape(STEP // 8, 8, BLOCK), axis=0)

    top = None
    for rows in parts:
        s = dot_nt(kv[h, 0, rows, :], query)
        b = bias[rows, :]
        s = s + jnp.concatenate([b] * (BLOCK // DIM), axis=1)
        score[rows, :] = s
        part = folded(s, jnp.max)
        top = part if top is None else jnp.maximum(top, part)
    top = jnp.max(top, axis=0, keepdims=True)
    norm = mixed = None
    for rows in parts:
        dp = dot_nt(kv[h, 1, rows, :], grad)
        e = jnp.exp2((score[rows, :] - top) * SCALE2)
        score[rows, :] = e
        dprob[rows, :] = dp
        part, other = folded(e, jnp.sum), folded(e * dp, jnp.sum)
        norm = part if norm is None else norm + part
        mixed = other if mixed is None else mixed + other
    inverse = 1.0 / jnp.sum(norm, axis=0, keepdims=True)
    delta = jnp.sum(mixed, axis=0, keepdims=True) * inverse
    for i, rows in enumerate(parts):
        p = score[rows, :] * inverse
        pb = p.astype(BF16)
        ds = (p * (dprob[rows, :] - delta)).astype(BF16)
        out, dq = dot_tn(kv[h, 1, rows, :], pb), dot_tn(kv[h, 0, rows, :], ds)
        if i == 0:
            total[0], total[1] = out, dq
        else:
            total[0] += out
            total[1] += dq
        dv, dk = dot_nn(pb, grad), dot_nn(ds, query) * SCALE
        if i * STEP < BLOCK:
            gown[h, 0, rows, :] = dk
            gown[h, 1, rows, :] = dv
        else:
            there = pl.ds(i * STEP - BLOCK, STEP)
            gset[h, 0, there, :] = dk.astype(BF16)
            gset[h, 1, there, :] = dv.astype(BF16)
    lanes = pl.ds(pl.multiple_of(h * DIM, DIM), DIM)
    att[:, lanes] = total[0].T.astype(BF16)
    gq[:, lanes] = (total[1].T * SCALE).astype(BF16)


def kernel(
    q_hbm, k_hbm, v_hbm, g_hbm, att, gq, gk, gv,
    kv, q_all, g_all, pooled, told, heard, gown, gset, pair, csend, cfar, cnear, clow,
    psend, rfar, rnear, rlow, level, lsend, hrecv, bias, mean, spread, score, dprob, total,
    send, recv, told_sem, heard_sem,
):
    g, s = lax.axis_index("grp"), lax.axis_index("seq")
    low, z = lax.div(g, 8), lax.rem(g, 8)
    high, x, core = lax.div(s, 8), lax.div(lax.rem(s, 8), 2), lax.rem(s, 2)
    other = 1 - core
    sibling = (g, s + 1 - 2 * core)
    across_hi = (g, (1 - high) * 8 + x * 2 + core)
    across_lo = ((1 - low) * 8 + z, s)
    slot_one = x * 4 + high * 2 + core
    slot_two = z * 2 + low
    has_prev = (g + s) > 0
    has_next = (g + s) < GROUPS + PLACES - 2
    up_group = lax.rem(g + lax.div(s + 1, PLACES), GROUPS)
    after = (up_group, lax.rem(s + 1, PLACES))
    low_group = lax.rem(g + GROUPS - 1 + lax.div(s + PLACES - 1, PLACES), GROUPS)
    before = (low_group, lax.rem(s + PLACES - 1, PLACES))

    def near_x(d):
        return lax.rem(x + d + 4, 4)

    def near_z(d):
        return lax.rem(z + d + 8, 8)

    def beside(d):
        return (g, high * 8 + near_x(d) * 2 + core)

    def along(d):
        return (low * 8 + near_z(d), s)

    def ranks(start, unit, count):
        return pl.ds(pl.multiple_of(start * unit, unit), count)

    def one_rows(column, row, count):
        return ranks(LEVEL1 // ONE + column * 4 + row * 2, ONE, count)

    def two_rows(column, row, count):
        return ranks(LEVEL2 // ONE + column * 2 + row, ONE, count)

    def heads(ch):
        return pl.ds(ch * PER, PER)

    def lanes(h):
        return pl.ds(pl.multiple_of(h * DIM, DIM), DIM)

    def push(transfer, ch, src, dst, device):
        pltpu.make_async_remote_copy(
            src_ref=src, dst_ref=dst, send_sem=send.at[transfer, ch], recv_sem=recv.at[transfer, ch],
            device_id=device, device_id_type=MESH,
        ).start()

    def await_rows(sems, transfer, ch, rows):
        ref = kv.at[heads(ch), 0, pl.ds(0, rows), :]
        pltpu.make_async_copy(ref, ref, sems.at[transfer, ch]).wait()

    def each_head(ch, do):
        lax.fori_loop(0, PER, lambda i, _: (do(ch * PER + i), 0)[1], 0)

    def each_peer(do):
        lax.fori_loop(1, PLACES, lambda j, _: (do(j), 0)[1], 0)

    def fetch(h, _):
        ch = lax.div(h, PER)
        for plane, src in enumerate((k_hbm, v_hbm)):
            pltpu.make_async_copy(
                src.at[:, lanes(h)], kv.at[h, plane, pl.ds(OWN, BLOCK), :], recv.at[IN_KV, ch]
            ).start()
        return 0

    def fetch_more(h, _):
        ch = lax.div(h, PER)
        for dst, src in ((q_all, q_hbm), (g_all, g_hbm)):
            pltpu.make_async_copy(src.at[:, lanes(h)], dst.at[h], recv.at[IN_QG, ch]).start()
        return 0

    lax.fori_loop(0, HEADS, fetch, 0)
    lax.fori_loop(0, HEADS, fetch_more, 0)

    barrier = pltpu.get_barrier_semaphore()

    def greet(j):
        for device in ((g, lax.rem(s + j, PLACES)), (lax.rem(g + j, GROUPS), s)):
            pl.semaphore_signal(barrier, inc=1, device_id=device, device_id_type=MESH)

    each_peer(greet)
    crosses_up = jnp.logical_and(s == PLACES - 1, has_next)
    crosses_down = jnp.logical_and(s == 0, has_prev)

    @pl.when(crosses_up)
    def _():
        pl.semaphore_signal(barrier, inc=1, device_id=after, device_id_type=MESH)

    @pl.when(crosses_down)
    def _():
        pl.semaphore_signal(barrier, inc=1, device_id=before, device_id_type=MESH)

    wide = (lax.broadcasted_iota(jnp.int32, (ONE, BLOCK), 0), lax.broadcasted_iota(jnp.int32, (ONE, BLOCK), 1))
    mean[...] = jnp.where(lax.shift_right_logical(wide[1], 4) == wide[0], 1.0 / POOL, 0.0).astype(BF16)
    tall = (lax.broadcasted_iota(jnp.int32, (BLOCK, ONE), 0), lax.broadcasted_iota(jnp.int32, (BLOCK, ONE), 1))
    spread[...] = jnp.where(lax.shift_right_logical(tall[0], 4) == tall[1], 1.0 / POOL, 0.0).astype(BF16)

    def pool_own(h, _):
        @pl.when(lax.rem(h, PER) == 0)
        def _():
            await_rows(recv, IN_KV, lax.div(h, PER), 2 * BLOCK)

        for plane in range(2):
            pooled[plane, h] = dot_nn(mean[...], kv[h, plane, pl.ds(OWN, BLOCK), :]).astype(BF16)
        kv[h, core, ranks(LEVEL1 // ONE + slot_one, ONE, ONE), :] = pooled[core, h]
        return 0

    lax.fori_loop(0, HEADS, pool_own, 0)
    told[...] = dot_nn(mean[...], pooled[...].reshape(2 * HEADS * ONE, DIM)).astype(BF16)
    heard[slot_one] = told[...]

    @pl.when(jnp.logical_not(has_prev))
    def _():
        kv[:, :, PREV:NEXT, :] = jnp.zeros((HEADS, 2, NEAR, DIM), BF16)
        hrecv[:, 0] = jnp.zeros((HEADS, 2, NEAR, DIM), BF16)

    @pl.when(jnp.logical_not(has_next))
    def _():
        kv[:, :, NEXT:LEVEL1, :] = jnp.zeros((HEADS, 2, NEAR, DIM), BF16)
        hrecv[:, 1] = jnp.zeros((HEADS, 2, NEAR, DIM), BF16)

    crosses = jnp.logical_or(crosses_up, crosses_down)

    @pl.when(crosses)
    def _():
        pl.semaphore_wait(barrier, PLACES + GROUPS - 1)

    @pl.when(jnp.logical_not(crosses))
    def _():
        pl.semaphore_wait(barrier, PLACES + GROUPS - 2)

    def tell(j):
        pltpu.make_async_remote_copy(
            src_ref=told, dst_ref=heard.at[slot_one], send_sem=told_sem.at[0], recv_sem=heard_sem.at[0],
            device_id=(g, lax.rem(s + j, PLACES)), device_id_type=MESH,
        ).start()

    each_peer(tell)

    def spread_rows(v):
        upper = v.astype(BF16)
        rest = (v - upper.astype(F32)).astype(BF16)
        return dot_nn(spread[...], upper) + dot_nn(spread[...], rest)

    def swap_pooled(ch):
        hs = heads(ch)
        push(PAIR_POOL, ch, pooled.at[other, hs], kv.at[hs, other, ranks(LEVEL1 // ONE + slot_one, ONE, ONE), :], sibling)

    def tables():
        row = lax.broadcasted_iota(jnp.int32, (SET, DIM), 0)
        slot = lax.shift_right_logical(row & (BLOCK - 1), 5)
        place = (lax.shift_right_logical(slot, 1) & 1) * 8 + lax.shift_right_logical(slot, 2) * 2 + (slot & 1)
        group = (slot & 1) * 8 + lax.shift_right_logical(slot, 1)
        dead_one = (row >= LEVEL1) & (row < LEVEL2) & (place >= s - 1) & (place <= s + 1)
        dead_two = (row >= LEVEL2) & (group == g)
        no_prev = (row >= PREV) & (row < NEXT) & (g + s == 0)
        no_next = (row >= NEXT) & (row < LEVEL1) & (g + s == GROUPS + PLACES - 2)
        bias[...] = jnp.where(dead_one | dead_two | no_prev | no_next, FILL, 0.0)

    def own_coarse():
        pltpu.make_async_copy(heard.at[pl.ds(0, PLACES - 1)], heard.at[pl.ds(0, PLACES - 1)], heard_sem.at[0]).wait()
        shape = (HEADS * ONE, PLACES * ONE)
        to, come = lax.broadcasted_iota(jnp.int32, shape, 0), lax.broadcasted_iota(jnp.int32, shape, 1)
        head, within = lax.shift_right_logical(to, 5), to & 31
        wanted = lax.shift_right_logical(within, 1) * ONE + core * 16 + head * 2 + (within & 1)
        pick = jnp.where(come == wanted, 1.0, 0.0).astype(BF16)
        rows = dot_nn(pick, heard[...].reshape(PLACES * ONE, DIM)).astype(BF16)
        for h in range(HEADS):
            kv[h, core, ranks(LEVEL2 // ONE + slot_two, ONE, ONE), :] = rows[h * ONE : (h + 1) * ONE]

    def swap_across(ch):
        hs = heads(ch)
        await_rows(recv, PAIR_POOL, ch, ONE)
        chip = kv.at[hs, core, one_rows(x, high, 2 * ONE), :]
        push(ACROSS_HI, ch, chip, chip, across_hi)

        @pl.when(ch == 0)
        def _():
            tables()
            own_coarse()

        group = kv.at[hs, core, two_rows(z, low, ONE), :]
        push(ACROSS_LO, ch, group, group, across_lo)

    def send_beside(ch):
        hs = heads(ch)
        await_rows(recv, ACROSS_HI, ch, 2 * ONE)
        column = kv.at[hs, core, one_rows(x, 0, 4 * ONE), :]
        push(RIGHT, ch, column, column, beside(1))
        push(LEFT, ch, column, column, beside(-1))
        await_rows(recv, ACROSS_LO, ch, ONE)
        both = kv.at[hs, core, two_rows(z, 0, 2 * ONE), :]
        for transfer, d in ((UP2, 2), (DOWN2, -2), (UP1, 1), (DOWN1, -1)):
            push(transfer, ch, both, both, along(d))

    def send_on(ch):
        hs = heads(ch)
        await_rows(recv, RIGHT, ch, 4 * ONE)
        part = kv.at[hs, core, one_rows(near_x(-1), 0, 2 * ONE), :]
        push(FAR_RIGHT, ch, part, part, beside(1))
        await_rows(recv, LEFT, ch, 4 * ONE)
        part = kv.at[hs, core, one_rows(near_x(1), 1, 2 * ONE), :]
        push(FAR_LEFT, ch, part, part, beside(-1))
        await_rows(recv, UP2, ch, 2 * ONE)
        both = kv.at[hs, core, two_rows(near_z(-2), 0, 2 * ONE), :]
        push(UP3, ch, both, both, along(1))
        part = kv.at[hs, core, two_rows(near_z(-2), 0, ONE), :]
        push(UP4, ch, part, part, along(2))
        await_rows(recv, DOWN2, ch, 2 * ONE)
        both = kv.at[hs, core, two_rows(near_z(2), 0, 2 * ONE), :]
        push(DOWN3, ch, both, both, along(-1))
        part = kv.at[hs, core, two_rows(near_z(2), 1, ONE), :]
        push(DOWN4, ch, part, part, along(-2))

        @pl.when(has_next)
        def _():
            push(FROM_PREV, ch, kv.at[hs, :, pl.ds(OWN + BLOCK - NEAR, NEAR), :], kv.at[hs, :, pl.ds(PREV, NEAR), :], after)

        @pl.when(has_prev)
        def _():
            push(FROM_NEXT, ch, kv.at[hs, :, pl.ds(OWN, NEAR), :], kv.at[hs, :, pl.ds(NEXT, NEAR), :], before)

    def swap_set(ch):
        hs = heads(ch)
        for transfer, rows in (
            (FAR_RIGHT, 2), (FAR_LEFT, 2), (UP1, 2), (DOWN1, 2), (UP3, 2), (DOWN3, 2), (UP4, 1), (DOWN4, 1),
        ):
            await_rows(recv, transfer, ch, rows * ONE)
        whole = kv.at[hs, core, pl.ds(LEVEL1, 2 * BLOCK), :]
        push(PAIR_SET, ch, whole, whole, sibling)

    def compute(ch):
        hs = heads(ch)
        await_rows(recv, IN_QG, ch, 2 * BLOCK)
        await_rows(recv, PAIR_SET, ch, 2 * BLOCK)

        @pl.when(has_prev)
        def _():
            await_rows(recv, FROM_PREV, ch, 2 * NEAR)

        @pl.when(has_next)
        def _():
            await_rows(recv, FROM_NEXT, ch, 2 * NEAR)

        each_head(
            ch,
            lambda h: attend(h, q_all, g_all, kv, bias, att, gq, gown, gset, score, dprob, total),
        )
        push(PAIR_GRAD, ch, gset.at[hs, other, pl.ds(LEVEL1 - BLOCK, 2 * BLOCK), :], pair.at[hs], sibling)

        @pl.when(has_prev)
        def _():
            push(GRAD_NEXT, ch, gset.at[hs, :, pl.ds(PREV - BLOCK, NEAR), :], hrecv.at[hs, 1], before)

        @pl.when(has_next)
        def _():
            push(GRAD_PREV, ch, gset.at[hs, :, pl.ds(NEXT - BLOCK, NEAR), :], hrecv.at[hs, 0], after)

    def added(a, b):
        return (a.astype(F32) + b.astype(F32)).astype(BF16)

    def group_rows(d, row, count):
        return ranks(near_z(d) * 2 + row, ONE, count)

    def place_rows(d, row, count):
        return ranks(near_x(d) * 4 + row * 2, ONE, count)

    def coarse_far(ch):
        hs = heads(ch)
        await_rows(recv, PAIR_GRAD, ch, 2 * BLOCK)

        def add(h):
            csend[h] = added(gset[h, core, pl.ds(LEVEL2 - BLOCK, BLOCK), :], pair[h, pl.ds(BLOCK, BLOCK), :])

        each_head(ch, add)
        push(C_DOWN4, ch, csend.at[hs, group_rows(-4, 0, ONE), :], cfar.at[hs, pl.ds(128, ONE), :], along(-2))
        push(C_UP4, ch, csend.at[hs, group_rows(4, 1, ONE), :], cfar.at[hs, pl.ds(160, ONE), :], along(2))
        push(C_DOWN3, ch, csend.at[hs, group_rows(-3, 0, 2 * ONE), :], cfar.at[hs, pl.ds(0, 64), :], along(-1))
        push(C_UP3, ch, csend.at[hs, group_rows(3, 0, 2 * ONE), :], cfar.at[hs, pl.ds(64, 64), :], along(1))

    def coarse_near(ch):
        hs = heads(ch)
        await_rows(recv, C_DOWN3, ch, 2 * ONE)
        await_rows(recv, C_UP3, ch, 2 * ONE)
        await_rows(recv, C_DOWN4, ch, ONE)
        await_rows(recv, C_UP4, ch, ONE)

        def add(h):
            for d, at, row, more in ((-2, 0, 0, 128), (2, 64, 1, 160)):
                for k in range(2):
                    rows = group_rows(d, k, ONE)
                    v = csend[h, rows, :].astype(F32) + cfar[h, pl.ds(at + k * ONE, ONE), :].astype(F32)
                    if k == row:
                        v = v + cfar[h, pl.ds(more, ONE), :].astype(F32)
                    csend[h, rows, :] = v.astype(BF16)

        each_head(ch, add)
        for i, (transfer, d) in enumerate(((C_UP2, 2), (C_DOWN2, -2), (C_UP1, 1), (C_DOWN1, -1))):
            push(transfer, ch, csend.at[hs, group_rows(d, 0, 64), :], cnear.at[hs, pl.ds(i * 64, 64), :], along(d))

    def coarse_low(ch):
        hs = heads(ch)
        for transfer in (C_UP2, C_DOWN2, C_UP1, C_DOWN1):
            await_rows(recv, transfer, ch, 2 * ONE)

        def add(h):
            rows = group_rows(0, 0, 64)
            v = csend[h, rows, :].astype(F32)
            for i in range(4):
                v = v + cnear[h, pl.ds(i * 64, 64), :].astype(F32)
            csend[h, rows, :] = v.astype(BF16)

        each_head(ch, add)
        push(C_LO, ch, csend.at[hs, group_rows(0, 1 - low, ONE), :], clow.at[hs], across_lo)

    def pool_far(ch):
        hs = heads(ch)
        await_rows(recv, C_LO, ch, ONE)

        def add(h):
            coarse = csend[h, group_rows(0, low, ONE), :].astype(F32) + clow[h].astype(F32)
            mine = gset[h, core, pl.ds(LEVEL1 - BLOCK, BLOCK), :].astype(F32)
            both = mine + pair[h, pl.ds(0, BLOCK), :].astype(F32)
            psend[h] = (both + spread_rows(coarse)).astype(BF16)

        each_head(ch, add)
        push(R_FAR_LEFT, ch, psend.at[hs, place_rows(-2, 0, 64), :], rfar.at[hs, pl.ds(0, 64), :], beside(-1))
        push(R_FAR_RIGHT, ch, psend.at[hs, place_rows(2, 1, 64), :], rfar.at[hs, pl.ds(64, 64), :], beside(1))

    def pool_near(ch):
        hs = heads(ch)
        await_rows(recv, R_FAR_LEFT, ch, 64)
        await_rows(recv, R_FAR_RIGHT, ch, 64)

        def add(h):
            for d, row in ((-1, 0), (1, 1)):
                rows = place_rows(d, row, 64)
                psend[h, rows, :] = added(psend[h, rows, :], rfar[h, pl.ds(row * 64, 64), :])

        each_head(ch, add)
        push(R_LEFT, ch, psend.at[hs, place_rows(-1, 0, 128), :], rnear.at[hs, pl.ds(0, 128), :], beside(-1))
        push(R_RIGHT, ch, psend.at[hs, place_rows(1, 0, 128), :], rnear.at[hs, pl.ds(128, 128), :], beside(1))

    def pool_high(ch):
        hs = heads(ch)
        await_rows(recv, R_LEFT, ch, 128)
        await_rows(recv, R_RIGHT, ch, 128)

        def add(h):
            rows = place_rows(0, 0, 128)
            v = psend[h, rows, :].astype(F32) + rnear[h, pl.ds(0, 128), :].astype(F32)
            psend[h, rows, :] = (v + rnear[h, pl.ds(128, 128), :].astype(F32)).astype(BF16)

        each_head(ch, add)
        push(R_HI, ch, psend.at[hs, place_rows(0, 1 - high, 64), :], rlow.at[hs], across_hi)

    def pool_pair(ch):
        hs = heads(ch)
        await_rows(recv, R_HI, ch, 64)

        def add(h):
            def sums(which):
                v = psend[h, ranks(x * 4 + high * 2 + which, ONE, ONE), :].astype(F32)
                return v + rlow[h, ranks(which, ONE, ONE), :].astype(F32)

            level[core, h] = sums(core)
            lsend[h] = sums(other)

        each_head(ch, add)
        push(R_PAIR, ch, lsend.at[hs], level.at[core, hs], sibling)

    def finish(ch):
        await_rows(recv, R_PAIR, ch, 2 * ONE)

        @pl.when(has_prev)
        def _():
            await_rows(recv, GRAD_PREV, ch, 2 * NEAR)

        @pl.when(has_next)
        def _():
            await_rows(recv, GRAD_NEXT, ch, 2 * NEAR)

        def add(h):
            for plane, dst in enumerate((gk, gv)):
                sums = gown[h, plane] + spread_rows(level[plane, h])
                for side in range(2):
                    rows = slice(side * NEAR, (side + 1) * NEAR)
                    dst[pl.ds(side * NEAR, NEAR), lanes(h)] = (
                        sums[rows] + hrecv[h, side, plane].astype(F32)
                    ).astype(BF16)

        each_head(ch, add)

    stages = (
        swap_pooled, swap_across, send_beside, send_on, swap_set, compute,
        coarse_far, coarse_near, coarse_low, pool_far, pool_near, pool_high, pool_pair, finish,
    )

    def step(t, _):
        for lag, stage in enumerate(stages):
            pl.when(jnp.logical_and(t >= lag, t < CHUNKS + lag))(functools.partial(stage, t - lag))
        return 0

    lax.fori_loop(0, CHUNKS + len(stages) - 1, step, 0)

    pltpu.make_async_copy(heard.at[pl.ds(0, PLACES - 1)], heard.at[pl.ds(0, PLACES - 1)], told_sem.at[0]).wait()

    def drain(ch, _):
        for rows, transfers in (
            (32, (PAIR_POOL, ACROSS_LO, UP4, DOWN4, C_DOWN4, C_UP4, C_LO)),
            (64, (ACROSS_HI, FAR_RIGHT, FAR_LEFT, UP1, DOWN1, UP2, DOWN2, UP3, DOWN3)),
            (64, (C_DOWN3, C_UP3, C_DOWN1, C_UP1, C_DOWN2, C_UP2, R_FAR_LEFT, R_FAR_RIGHT, R_HI, R_PAIR)),
            (128, (RIGHT, LEFT, R_LEFT, R_RIGHT)),
            (1024, (PAIR_SET, PAIR_GRAD)),
        ):
            for transfer in transfers:
                await_rows(send, transfer, ch, rows)

        @pl.when(has_prev)
        def _():
            await_rows(send, FROM_NEXT, ch, 2 * NEAR)
            await_rows(send, GRAD_NEXT, ch, 2 * NEAR)

        @pl.when(has_next)
        def _():
            await_rows(send, FROM_PREV, ch, 2 * NEAR)
            await_rows(send, GRAD_PREV, ch, 2 * NEAR)

        return 0

    lax.fori_loop(0, CHUNKS, drain, 0)


def body(query_rows, key_rows, value_rows, grad_out):
    shape = jax.ShapeDtypeStruct(query_rows.shape, BF16)

    def rows(count, *lead):
        return ((*lead, HEADS, count, DIM), BF16)

    scratch = [
        ((HEADS, 2, SET, DIM), BF16),
        rows(BLOCK),
        rows(BLOCK),
        rows(ONE, 2),
        ((ONE, DIM), BF16),
        ((PLACES, ONE, DIM), BF16),
        ((HEADS, 2, BLOCK, DIM), F32),
        ((HEADS, 2, SET - BLOCK, DIM), BF16),
        rows(2 * BLOCK),
        rows(BLOCK),
        rows(192),
        rows(256),
        rows(ONE),
        rows(BLOCK),
        rows(128),
        rows(256),
        rows(64),
        ((2, HEADS, ONE, DIM), F32),
        ((HEADS, ONE, DIM), F32),
        ((HEADS, 2, 2, NEAR, DIM), BF16),
        ((SET, DIM), F32),
        ((ONE, BLOCK), BF16),
        ((BLOCK, ONE), BF16),
        ((SET, BLOCK), F32),
        ((SET, BLOCK), F32),
        ((2, DIM, BLOCK), F32),
    ]
    anywhere = pl.BlockSpec(memory_space=pl.ANY)
    return pl.pallas_call(
        kernel,
        out_shape=[shape] * 4,
        in_specs=[anywhere] * 4,
        out_specs=[pl.BlockSpec(memory_space=pltpu.VMEM)] * 4,
        scratch_shapes=[pltpu.VMEM(*one) for one in scratch]
        + [pltpu.SemaphoreType.DMA((TRANSFERS, CHUNKS))] * 2
        + [pltpu.SemaphoreType.DMA((1,))] * 2,
        compiler_params=pltpu.CompilerParams(
            collective_id=0, has_side_effects=True, vmem_limit_bytes=58 << 20
        ),
        name="hierarchical",
    )(query_rows, key_rows, value_rows, grad_out)


def solution(mesh):
    placed = P(("grp", "seq"), None)
    return jax.shard_map(
        body, mesh=mesh, in_specs=(placed,) * 4, out_specs=(placed,) * 4, check_vma=False
    )
```

time: 114 us -> 115 us (level)
  no operation moved by 1% of the time
where the time goes in v2:
time: 115 us; the launch traced here: 114 us
  Pallas kernels  107 us (93%)
  local copies, waits for them, and re-layouts  6.53 us (6%)
    pallas_call x1, Pallas kernels, body(): pl.pallas_call(kernel, out_shape=[shape] * 4, in_specs=[anywhere] * 4, ou...  107 us
    unnamed x10, local copies, waits for them, and re-layouts  6.53 us

profile of v2, /device:TPU:1, one launch (start us, length us, event | category | flops | bytes accessed | tf_op | source)
XLA Modules:
  0.0 114.4 jit_solution(5954026598646595110)
XLA Ops:
  0.6 107.2 %hierarchical.1 = (bf16[512,1024]{1,0:T(8,128)(2,1)}, bf16[512,1024]{1,0:T(8,128)(2,1)}, bf16[512,1024]{1,0:T(8,128)(2,1)}, bf16[512,1024]{1,0:T(8,128)(2,1)}) custom-call(bf16[512,1024]{1,0:T(8,128)(2,1)} %q_hbm.1, bf16[512,1024]{1,0:T(8,128)(2,1)} %k_hbm.1, bf16[512,1024]{1,0:T(8,128)(2,1)} %v_hbm.1, bf16[512,1024]{1,0:T(8,128)(2,1)} %g_hbm.1), custom_call_target="tpu_custom_call" | custom-call | tf_op jit(solution)/shard_map/hierarchical/pallas_call | solution.py:579
  107.8 0.0 copy-start.2
  107.9 2.4 %copy.12 = bf16[512,1024]{1,0:T(8,128)(2,1)} copy(bf16[512,1024]{1,0:T(8,128)(2,1)} %get-tuple-element.8) | data formatting | bytes 2097152
  110.2 0.0 copy-done.2
  110.2 0.0 copy-start.1
  110.2 1.0 copy.13
  111.2 0.6 copy-done.1
  111.8 0.0 copy-start
  111.8 1.0 copy.14
  112.8 0.6 copy-done
  113.4 1.0 copy.15
Async XLA Ops:
  107.8 2.4 %copy-start.2 = (bf16[512,1024]{1,0:T(8,128)(2,1)S(1)}, bf16[512,1024]{1,0:T(8,128)(2,1)}, u32[]{:S(2)}) copy-start(bf16[512,1024]{1,0:T(8,128)(2,1)} %get-tuple-element.9) | copy-start | bytes 3145732
  110.2 1.6 %copy-start.1 = (bf16[512,1024]{1,0:T(8,128)(2,1)S(1)}, bf16[512,1024]{1,0:T(8,128)(2,1)}, u32[]{:S(2)}) copy-start(bf16[512,1024]{1,0:T(8,128)(2,1)} %get-tuple-element.10) | copy-start | bytes 3145732
  111.8 1.6 %copy-start = (bf16[512,1024]{1,0:T(8,128)(2,1)S(1)}, bf16[512,1024]{1,0:T(8,128)(2,1)}, u32[]{:S(2)}) copy-start(bf16[512,1024]{1,0:T(8,128)(2,1)} %get-tuple-element.11) | copy-start | bytes 3145732

commit v3 on v2

v3 whole, which is shorter than its diff:
```python
import functools

import jax
import jax.numpy as jnp
from jax import lax
from jax.experimental import pallas as pl
from jax.experimental.pallas import tpu as pltpu
from jax.sharding import PartitionSpec as P

F32 = jnp.float32
BF16 = jnp.bfloat16
HEADS = 8
DIM = 128
BLOCK = 512
NEAR = 256
POOL = 16
ONE = BLOCK // POOL
TWO = ONE // POOL
PLACES = 16
GROUPS = 16
SET = 2048
OWN, PREV, NEXT, LEVEL1, LEVEL2 = 0, 512, 768, 1024, 1536
SCALE = DIM**-0.5
SCALE2 = SCALE * 1.4426950408889634
FILL = -1e30
MESH = pl.DeviceIdType.MESH
CHUNKS = 8
PER = HEADS // CHUNKS
STEP = 512

IN_KV, IN_QG, COLUMN, BESIDE, ALONG, PAIR_SET, FROM_PREV = range(0, 7)
FROM_NEXT, PAIR_GRAD, GRAD_PREV, GRAD_NEXT, ALONG_GRAD, BESIDE_GRAD, COLUMN_GRAD = range(7, 14)
TRANSFERS = 14


def dot_nt(a, b):
    return lax.dot_general(a, b, (((1,), (1,)), ((), ())), preferred_element_type=F32)


def dot_tn(a, b):
    return lax.dot_general(a, b, (((0,), (0,)), ((), ())), preferred_element_type=F32)


def dot_nn(a, b):
    return jnp.dot(a, b, preferred_element_type=F32)


def attend(h, q_all, g_all, kv, bias, att, gq, gown, gset, score, dprob, total):
    query, grad = q_all[h], g_all[h]
    parts = [pl.ds(i * STEP, STEP) for i in range(SET // STEP)]

    def folded(x, op):
        return op(x.reshape(STEP // 8, 8, BLOCK), axis=0)

    top = None
    for rows in parts:
        s = dot_nt(kv[h, 0, rows, :], query)
        b = bias[rows, :]
        s = s + jnp.concatenate([b] * (BLOCK // DIM), axis=1)
        score[rows, :] = s
        part = folded(s, jnp.max)
        top = part if top is None else jnp.maximum(top, part)
    top = jnp.max(top, axis=0, keepdims=True)
    norm = mixed = None
    for rows in parts:
        dp = dot_nt(kv[h, 1, rows, :], grad)
        e = jnp.exp2((score[rows, :] - top) * SCALE2)
        score[rows, :] = e
        dprob[rows, :] = dp
        part, other = folded(e, jnp.sum), folded(e * dp, jnp.sum)
        norm = part if norm is None else norm + part
        mixed = other if mixed is None else mixed + other
    inverse = 1.0 / jnp.sum(norm, axis=0, keepdims=True)
    delta = jnp.sum(mixed, axis=0, keepdims=True) * inverse
    for i, rows in enumerate(parts):
        p = score[rows, :] * inverse
        pb = p.astype(BF16)
        ds = (p * (dprob[rows, :] - delta)).astype(BF16)
        out, dq = dot_tn(kv[h, 1, rows, :], pb), dot_tn(kv[h, 0, rows, :], ds)
        if i == 0:
            total[0], total[1] = out, dq
        else:
            total[0] += out
            total[1] += dq
        dv, dk = dot_nn(pb, grad), dot_nn(ds, query) * SCALE
        if i * STEP < BLOCK:
            gown[h, 0, rows, :] = dk
            gown[h, 1, rows, :] = dv
        else:
            there = pl.ds(i * STEP - BLOCK, STEP)
            gset[h, 0, there, :] = dk.astype(BF16)
            gset[h, 1, there, :] = dv.astype(BF16)
    lanes = pl.ds(pl.multiple_of(h * DIM, DIM), DIM)
    att[:, lanes] = total[0].T.astype(BF16)
    gq[:, lanes] = (total[1].T * SCALE).astype(BF16)


def kernel(
    q_hbm, k_hbm, v_hbm, g_hbm, att, gq, gk, gv,
    kv, q_all, g_all, pooled, told, heard, gown, gset, pair, csend, cin, csum, psend, pin, asend, ain,
    tsend, tin, hrecv, bias, mean, spread, score, dprob, total,
    send, recv, small_send, small_recv,
):
    g, s = lax.axis_index("grp"), lax.axis_index("seq")
    low, z = lax.div(g, 8), lax.rem(g, 8)
    high, x, core = lax.div(s, 8), lax.div(lax.rem(s, 8), 2), lax.rem(s, 2)
    other = 1 - core
    sibling = (g, s + 1 - 2 * core)
    slot_one = x * 4 + high * 2 + core
    has_prev = (g + s) > 0
    has_next = (g + s) < GROUPS + PLACES - 2
    up_group = lax.rem(g + lax.div(s + 1, PLACES), GROUPS)
    after = (up_group, lax.rem(s + 1, PLACES))
    low_group = lax.rem(g + GROUPS - 1 + lax.div(s + PLACES - 1, PLACES), GROUPS)
    before = (low_group, lax.rem(s + PLACES - 1, PLACES))

    def near_x(d):
        return lax.rem(x + d + 4, 4)

    def near_z(d):
        return lax.rem(z + d + 8, 8)

    def beside(d):
        return (g, high * 8 + near_x(d) * 2 + core)

    def along(d):
        return (low * 8 + near_z(d), s)

    def ranks(start, unit, count):
        return pl.ds(pl.multiple_of(start * unit, unit), count)

    def one_rows(column, row, count):
        return ranks(LEVEL1 // ONE + column * 4 + row * 2, ONE, count)

    def two_rows(column, row, count):
        return ranks(LEVEL2 // ONE + column * 2 + row, ONE, count)

    def heads(ch):
        return pl.ds(ch * PER, PER)

    def lanes(h):
        return pl.ds(pl.multiple_of(h * DIM, DIM), DIM)

    def push(transfer, ch, src, dst, device):
        pltpu.make_async_remote_copy(
            src_ref=src, dst_ref=dst, send_sem=send.at[transfer, ch], recv_sem=recv.at[transfer, ch],
            device_id=device, device_id_type=MESH,
        ).start()

    def await_rows(sems, transfer, ch, rows):
        ref = kv.at[heads(ch), 0, pl.ds(0, rows), :]
        pltpu.make_async_copy(ref, ref, sems.at[transfer, ch]).wait()

    def each_head(ch, do):
        lax.fori_loop(0, PER, lambda i, _: (do(ch * PER + i), 0)[1], 0)

    def fetch(h, _):
        ch = lax.div(h, PER)
        for plane, src in enumerate((k_hbm, v_hbm)):
            pltpu.make_async_copy(
                src.at[:, lanes(h)], kv.at[h, plane, pl.ds(OWN, BLOCK), :], recv.at[IN_KV, ch]
            ).start()
        return 0

    def fetch_more(h, _):
        ch = lax.div(h, PER)
        for dst, src in ((q_all, q_hbm), (g_all, g_hbm)):
            pltpu.make_async_copy(src.at[:, lanes(h)], dst.at[h], recv.at[IN_QG, ch]).start()
        return 0

    lax.fori_loop(0, HEADS, fetch, 0)
    lax.fori_loop(0, HEADS, fetch_more, 0)

    barrier = pltpu.get_barrier_semaphore()

    def meet(device):
        pl.semaphore_signal(barrier, inc=1, device_id=device, device_id_type=MESH)

    def column_peer(j):
        rank = lax.rem(low * PLACES + s + j, 2 * PLACES)
        return lax.div(rank, PLACES), lax.rem(rank, PLACES)

    def greet(j, _):
        half, place = column_peer(j)
        meet((half * 8 + z, place))
        return 0

    lax.fori_loop(1, 2 * PLACES, greet, 0)
    lax.fori_loop(1, 8, lambda d, _: (meet(along(d)), 0)[1], 0)
    crosses_up = jnp.logical_and(s == PLACES - 1, has_next)
    crosses_down = jnp.logical_and(s == 0, has_prev)

    @pl.when(crosses_up)
    def _():
        pl.semaphore_signal(barrier, inc=1, device_id=after, device_id_type=MESH)

    @pl.when(crosses_down)
    def _():
        pl.semaphore_signal(barrier, inc=1, device_id=before, device_id_type=MESH)

    wide = (lax.broadcasted_iota(jnp.int32, (ONE, BLOCK), 0), lax.broadcasted_iota(jnp.int32, (ONE, BLOCK), 1))
    mean[...] = jnp.where(lax.shift_right_logical(wide[1], 4) == wide[0], 1.0 / POOL, 0.0).astype(BF16)
    tall = (lax.broadcasted_iota(jnp.int32, (BLOCK, ONE), 0), lax.broadcasted_iota(jnp.int32, (BLOCK, ONE), 1))
    spread[...] = jnp.where(lax.shift_right_logical(tall[0], 4) == tall[1], 1.0 / POOL, 0.0).astype(BF16)

    def pool_own(h, _):
        @pl.when(lax.rem(h, PER) == 0)
        def _():
            await_rows(recv, IN_KV, lax.div(h, PER), 2 * BLOCK)

        for plane in range(2):
            pooled[plane, h] = dot_nn(mean[...], kv[h, plane, pl.ds(OWN, BLOCK), :]).astype(BF16)
        kv[h, core, ranks(LEVEL1 // ONE + slot_one, ONE, ONE), :] = pooled[core, h]
        return 0

    lax.fori_loop(0, HEADS, pool_own, 0)
    told[...] = dot_nn(mean[...], pooled[...].reshape(2 * HEADS * ONE, DIM)).astype(BF16)
    heard[low * PLACES + slot_one] = told[...]

    @pl.when(jnp.logical_not(has_prev))
    def _():
        kv[:, :, PREV:NEXT, :] = jnp.zeros((HEADS, 2, NEAR, DIM), BF16)
        hrecv[:, 0] = jnp.zeros((HEADS, 2, NEAR, DIM), BF16)

    @pl.when(jnp.logical_not(has_next))
    def _():
        kv[:, :, NEXT:LEVEL1, :] = jnp.zeros((HEADS, 2, NEAR, DIM), BF16)
        hrecv[:, 1] = jnp.zeros((HEADS, 2, NEAR, DIM), BF16)

    crosses = jnp.logical_or(crosses_up, crosses_down)

    @pl.when(crosses)
    def _():
        pl.semaphore_wait(barrier, 2 * PLACES - 1 + 7 + 1)

    @pl.when(jnp.logical_not(crosses))
    def _():
        pl.semaphore_wait(barrier, 2 * PLACES - 1 + 7)

    def tell(j, _):
        half, place = column_peer(j)
        pltpu.make_async_remote_copy(
            src_ref=told, dst_ref=heard.at[low * PLACES + slot_one],
            send_sem=small_send.at[0], recv_sem=small_recv.at[0],
            device_id=(half * 8 + z, place), device_id_type=MESH,
        ).start()
        return 0

    lax.fori_loop(1, 2 * PLACES, tell, 0)

    def await_small(sems, which, ref):
        pltpu.make_async_copy(ref, ref, sems.at[which]).wait()

    def spread_rows(v):
        upper = v.astype(BF16)
        rest = (v - upper.astype(F32)).astype(BF16)
        return dot_nn(spread[...], upper) + dot_nn(spread[...], rest)

    def tables():
        row = lax.broadcasted_iota(jnp.int32, (SET, DIM), 0)
        slot = lax.shift_right_logical(row & (BLOCK - 1), 5)
        place = (lax.shift_right_logical(slot, 1) & 1) * 8 + lax.shift_right_logical(slot, 2) * 2 + (slot & 1)
        group = (slot & 1) * 8 + lax.shift_right_logical(slot, 1)
        dead_one = (row >= LEVEL1) & (row < LEVEL2) & (place >= s - 1) & (place <= s + 1)
        dead_two = (row >= LEVEL2) & (group == g)
        no_prev = (row >= PREV) & (row < NEXT) & (g + s == 0)
        no_next = (row >= NEXT) & (row < LEVEL1) & (g + s == GROUPS + PLACES - 2)
        bias[...] = jnp.where(dead_one | dead_two | no_prev | no_next, FILL, 0.0)

    def own_coarse():
        await_small(small_recv, 0, heard.at[pl.ds(0, 2 * PLACES - 1)])
        shape = (HEADS * ONE, PLACES * ONE)
        to, come = lax.broadcasted_iota(jnp.int32, shape, 0), lax.broadcasted_iota(jnp.int32, shape, 1)
        head, within = lax.shift_right_logical(to, 5), to & 31
        wanted = lax.shift_right_logical(within, 1) * ONE + core * 16 + head * 2 + (within & 1)
        pick = jnp.where(come == wanted, 1.0, 0.0).astype(BF16)
        for half in range(2):
            there = heard[half * PLACES : (half + 1) * PLACES].reshape(PLACES * ONE, DIM)
            rows = dot_nn(pick, there).astype(BF16)
            for h in range(HEADS):
                kv[h, core, two_rows(z, half, ONE), :] = rows[h * ONE : (h + 1) * ONE]

    def column(which):
        return (g, (1 - high) * 8 + x * 2 + which)

    def send_column(ch):
        hs = heads(ch)
        mine = ranks(LEVEL1 // ONE + slot_one, ONE, ONE)
        for plane in range(2):
            push(COLUMN, ch, pooled.at[plane, hs], kv.at[hs, plane, mine, :], column(plane))
        push(COLUMN, ch, pooled.at[other, hs], kv.at[hs, other, mine, :], sibling)

    def send_planes(ch):
        hs = heads(ch)
        await_rows(recv, COLUMN, ch, 3 * ONE)
        rows = kv.at[hs, core, one_rows(x, 0, 4 * ONE), :]
        for d in (2, 1, 3):
            push(BESIDE, ch, rows, rows, beside(d))

        @pl.when(ch == 0)
        def _():
            own_coarse()

        both = kv.at[hs, core, two_rows(z, 0, 2 * ONE), :]
        for d in (4, 3, 5, 2, 6, 1, 7):
            push(ALONG, ch, both, both, along(d))

        @pl.when(has_next)
        def _():
            push(FROM_PREV, ch, kv.at[hs, :, pl.ds(OWN + BLOCK - NEAR, NEAR), :], kv.at[hs, :, pl.ds(PREV, NEAR), :], after)

        @pl.when(has_prev)
        def _():
            push(FROM_NEXT, ch, kv.at[hs, :, pl.ds(OWN, NEAR), :], kv.at[hs, :, pl.ds(NEXT, NEAR), :], before)

        @pl.when(ch == 0)
        def _():
            tables()

    def swap_set(ch):
        hs = heads(ch)
        await_rows(recv, BESIDE, ch, 12 * ONE)
        await_rows(recv, ALONG, ch, 14 * ONE)
        whole = kv.at[hs, core, pl.ds(LEVEL1, 2 * BLOCK), :]
        push(PAIR_SET, ch, whole, whole, sibling)

    def compute(ch):
        hs = heads(ch)
        await_rows(recv, IN_QG, ch, 2 * BLOCK)
        await_rows(recv, PAIR_SET, ch, 2 * BLOCK)

        @pl.when(has_prev)
        def _():
            await_rows(recv, FROM_PREV, ch, 2 * NEAR)

        @pl.when(has_next)
        def _():
            await_rows(recv, FROM_NEXT, ch, 2 * NEAR)

        each_head(
            ch,
            lambda h: attend(h, q_all, g_all, kv, bias, att, gq, gown, gset, score, dprob, total),
        )
        push(PAIR_GRAD, ch, gset.at[hs, other, pl.ds(LEVEL1 - BLOCK, 2 * BLOCK), :], pair.at[hs], sibling)

        @pl.when(has_prev)
        def _():
            push(GRAD_NEXT, ch, gset.at[hs, :, pl.ds(PREV - BLOCK, NEAR), :], hrecv.at[hs, 1], before)

        @pl.when(has_next)
        def _():
            push(GRAD_PREV, ch, gset.at[hs, :, pl.ds(NEXT - BLOCK, NEAR), :], hrecv.at[hs, 0], after)

    def added(a, b):
        return (a.astype(F32) + b.astype(F32)).astype(BF16)

    def send_grads(ch):
        hs = heads(ch)
        await_rows(recv, PAIR_GRAD, ch, 2 * BLOCK)

        def add(h):
            psend[h] = added(gset[h, core, pl.ds(LEVEL1 - BLOCK, BLOCK), :], pair[h, pl.ds(0, BLOCK), :])
            csend[h] = added(gset[h, core, pl.ds(LEVEL2 - BLOCK, BLOCK), :], pair[h, pl.ds(BLOCK, BLOCK), :])

        each_head(ch, add)
        for d in (2, 1, 3):
            push(
                BESIDE_GRAD, ch, psend.at[hs, ranks(near_x(d), 128, 128), :],
                pin.at[hs, ranks(x, 128, 128), :], beside(d),
            )
        for d in (4, 3, 5, 2, 6, 1, 7):
            push(
                ALONG_GRAD, ch, csend.at[hs, ranks(near_z(d), 64, 64), :],
                cin.at[hs, ranks(z, 64, 64), :], along(d),
            )

    def column_grads(ch):
        hs = heads(ch)
        await_rows(recv, BESIDE_GRAD, ch, 12 * ONE)

        def add(h):
            v = psend[h, ranks(x, 128, 128), :].astype(F32)
            for d in range(1, 4):
                v = v + pin[h, ranks(near_x(d), 128, 128), :].astype(F32)
            asend[h] = v.astype(BF16)
            ain[h, ranks(core * 2 + high, ONE, ONE), :] = asend[h, ranks(high * 2 + core, ONE, ONE), :]

        each_head(ch, add)
        place = ain.at[hs, ranks(core * 2 + high, ONE, ONE), :]
        for which in range(2):
            push(
                COLUMN_GRAD, ch, asend.at[hs, ranks((1 - high) * 2 + which, ONE, ONE), :], place,
                column(which),
            )
        push(COLUMN_GRAD, ch, asend.at[hs, ranks(high * 2 + other, ONE, ONE), :], place, sibling)
        await_rows(recv, ALONG_GRAD, ch, 14 * ONE)

        def add_coarse(h):
            v = csend[h, ranks(z, 64, 64), :].astype(F32)
            for d in range(1, 8):
                v = v + cin[h, ranks(near_z(d), 64, 64), :].astype(F32)
            csum[h] = v.astype(BF16)

        each_head(ch, add_coarse)

    def finish(ch):
        await_rows(recv, COLUMN_GRAD, ch, 3 * ONE)

        @pl.when(has_prev)
        def _():
            await_rows(recv, GRAD_PREV, ch, 2 * NEAR)

        @pl.when(has_next)
        def _():
            await_rows(recv, GRAD_NEXT, ch, 2 * NEAR)

        def add(h):
            for plane in range(2):
                level = ain[h, pl.ds(2 * plane * ONE, ONE), :].astype(F32)
                level = level + ain[h, pl.ds((2 * plane + 1) * ONE, ONE), :].astype(F32)
                sums = gown[h, plane] + spread_rows(level)
                for side in range(2):
                    rows = slice(side * NEAR, (side + 1) * NEAR)
                    gown[h, plane, rows, :] = sums[rows] + hrecv[h, side, plane].astype(F32)

        each_head(ch, add)

    stages = (send_column, send_planes, swap_set, compute, send_grads, column_grads, finish)

    def step(t, _):
        for lag, stage in enumerate(stages):
            pl.when(jnp.logical_and(t >= lag, t < CHUNKS + lag))(functools.partial(stage, t - lag))

        @pl.when(t == CHUNKS + 4)
        def _():
            send_coarse_sums()

        return 0

    def send_coarse_sums():
        shape = (BLOCK, BLOCK)
        to, come = lax.broadcasted_iota(jnp.int32, shape, 0), lax.broadcasted_iota(jnp.int32, shape, 1)
        target, within = lax.shift_right_logical(to, 4), to & 15
        wanted = lax.shift_right_logical(within, 1) * 64 + target * 2 + (within & 1)
        pick = jnp.where(come == wanted, 1.0, 0.0).astype(BF16)
        tsend[...] = dot_nn(pick, csum[...].reshape(BLOCK, DIM)).astype(BF16)
        source = low * 8 + high * 4 + x
        tin[core, source] = tsend[ranks(low * PLACES + slot_one, 16, 16), :]

        def tell_sums(j, _):
            half, place = column_peer(j)
            slot = lax.div(lax.rem(place, 8), 2) * 4 + lax.div(place, 8) * 2 + lax.rem(place, 2)
            pltpu.make_async_remote_copy(
                src_ref=tsend.at[ranks(half * PLACES + slot, 16, 16), :], dst_ref=tin.at[core, source],
                send_sem=small_send.at[1], recv_sem=small_recv.at[1],
                device_id=(half * 8 + z, place), device_id_type=MESH,
            ).start()
            return 0

        lax.fori_loop(1, 2 * PLACES, tell_sums, 0)

    lax.fori_loop(0, CHUNKS + len(stages) - 1, step, 0)

    sums_in = tsend.at[pl.ds(0, (2 * PLACES - 1) * 16), :]
    await_small(small_recv, 1, sums_in)
    for plane, dst in enumerate((gk, gv)):
        coarse = tin[plane, 0].astype(F32)
        for i in range(1, 16):
            coarse = coarse + tin[plane, i].astype(F32)
        coarse = coarse * (1.0 / (POOL * POOL))
        for h in range(HEADS):
            for side in range(2):
                rows = slice(side * NEAR, (side + 1) * NEAR)
                row = coarse[2 * h + side : 2 * h + side + 1]
                dst[rows, h * DIM : (h + 1) * DIM] = (gown[h, plane, rows, :] + row).astype(BF16)

    await_small(small_send, 0, heard.at[pl.ds(0, 2 * PLACES - 1)])
    await_small(small_send, 1, sums_in)

    def drain(ch, _):
        for transfer, rows in (
            (COLUMN, 96), (BESIDE, 384), (ALONG, 448), (PAIR_SET, 1024),
            (PAIR_GRAD, 1024), (ALONG_GRAD, 448), (BESIDE_GRAD, 384), (COLUMN_GRAD, 96),
        ):
            await_rows(send, transfer, ch, rows)

        @pl.when(has_prev)
        def _():
            await_rows(send, FROM_NEXT, ch, 2 * NEAR)
            await_rows(send, GRAD_NEXT, ch, 2 * NEAR)

        @pl.when(has_next)
        def _():
            await_rows(send, FROM_PREV, ch, 2 * NEAR)
            await_rows(send, GRAD_PREV, ch, 2 * NEAR)

        return 0

    lax.fori_loop(0, CHUNKS, drain, 0)


def body(query_rows, key_rows, value_rows, grad_out):
    shape = jax.ShapeDtypeStruct(query_rows.shape, BF16)

    def rows(count, *lead):
        return ((*lead, HEADS, count, DIM), BF16)

    scratch = [
        ((HEADS, 2, SET, DIM), BF16),
        rows(BLOCK),
        rows(BLOCK),
        rows(ONE, 2),
        ((ONE, DIM), BF16),
        ((2 * PLACES, ONE, DIM), BF16),
        ((HEADS, 2, BLOCK, DIM), F32),
        ((HEADS, 2, SET - BLOCK, DIM), BF16),
        rows(2 * BLOCK),
        rows(BLOCK),
        rows(BLOCK),
        rows(64),
        rows(BLOCK),
        rows(BLOCK),
        rows(128),
        rows(128),
        ((BLOCK, DIM), BF16),
        ((2, 16, 16, DIM), BF16),
        ((HEADS, 2, 2, NEAR, DIM), BF16),
        ((SET, DIM), F32),
        ((ONE, BLOCK), BF16),
        ((BLOCK, ONE), BF16),
        ((SET, BLOCK), F32),
        ((SET, BLOCK), F32),
        ((2, DIM, BLOCK), F32),
    ]
    anywhere = pl.BlockSpec(memory_space=pl.ANY)
    return pl.pallas_call(
        kernel,
        out_shape=[shape] * 4,
        in_specs=[anywhere] * 4,
        out_specs=[pl.BlockSpec(memory_space=pltpu.VMEM)] * 4,
        scratch_shapes=[pltpu.VMEM(*one) for one in scratch]
        + [pltpu.SemaphoreType.DMA((TRANSFERS, CHUNKS))] * 2
        + [pltpu.SemaphoreType.DMA((2,))] * 2,
        compiler_params=pltpu.CompilerParams(
            collective_id=0, has_side_effects=True, vmem_limit_bytes=58 << 20
        ),
        name="hierarchical",
    )(query_rows, key_rows, value_rows, grad_out)


def solution(mesh):
    placed = P(("grp", "seq"), None)
    return jax.shard_map(
        body, mesh=mesh, in_specs=(placed,) * 4, out_specs=(placed,) * 4, check_vma=False
    )
```

time: 115 us -> 110 us (0.957)
  Pallas kernels: 107 us -> 102 us
    pallas_call x1, Pallas kernels: 107 us -> 102 us  [body(): pl.pallas_call(kernel, out_shape=[shape] * 4, in_specs=[anywhere] * 4, ou...]
where the time goes in v3:
time: 110 us
  Pallas kernels  102 us (93%)
  local copies, waits for them, and re-layouts  6.53 us (6%)
    pallas_call x1, Pallas kernels, body(): pl.pallas_call(kernel, out_shape=[shape] * 4, in_specs=[anywhere] * 4, ou...  102 us
    unnamed x10, local copies, waits for them, and re-layouts  6.53 us

profile of v3, /device:TPU:1, one launch (start us, length us, event | category | flops | bytes accessed | tf_op | source)
XLA Modules:
  0.0 109.6 jit_solution(11381284917506743058)
XLA Ops:
  0.6 102.4 %hierarchical.1 = (bf16[512,1024]{1,0:T(8,128)(2,1)}, bf16[512,1024]{1,0:T(8,128)(2,1)}, bf16[512,1024]{1,0:T(8,128)(2,1)}, bf16[512,1024]{1,0:T(8,128)(2,1)}) custom-call(bf16[512,1024]{1,0:T(8,128)(2,1)} %q_hbm.1, bf16[512,1024]{1,0:T(8,128)(2,1)} %k_hbm.1, bf16[512,1024]{1,0:T(8,128)(2,1)} %v_hbm.1, bf16[512,1024]{1,0:T(8,128)(2,1)} %g_hbm.1), custom_call_target="tpu_custom_call" | custom-call | tf_op jit(solution)/shard_map/hierarchical/pallas_call | solution.py:536
  103.0 0.0 copy-start.2
  103.0 2.4 %copy.12 = bf16[512,1024]{1,0:T(8,128)(2,1)} copy(bf16[512,1024]{1,0:T(8,128)(2,1)} %get-tuple-element.8) | data formatting | bytes 2097152
  105.4 0.0 copy-done.2
  105.4 0.0 copy-start.1
  105.4 1.0 copy.13
  106.4 0.6 copy-done.1
  107.0 0.0 copy-start
  107.0 1.0 copy.14
  108.0 0.6 copy-done
  108.6 1.0 copy.15
Async XLA Ops:
  103.0 2.4 %copy-start.2 = (bf16[512,1024]{1,0:T(8,128)(2,1)S(1)}, bf16[512,1024]{1,0:T(8,128)(2,1)}, u32[]{:S(2)}) copy-start(bf16[512,1024]{1,0:T(8,128)(2,1)} %get-tuple-element.9) | copy-start | bytes 3145732
  105.4 1.6 %copy-start.1 = (bf16[512,1024]{1,0:T(8,128)(2,1)S(1)}, bf16[512,1024]{1,0:T(8,128)(2,1)}, u32[]{:S(2)}) copy-start(bf16[512,1024]{1,0:T(8,128)(2,1)} %get-tuple-element.10) | copy-start | bytes 3145732
  107.0 1.6 %copy-start = (bf16[512,1024]{1,0:T(8,128)(2,1)S(1)}, bf16[512,1024]{1,0:T(8,128)(2,1)}, u32[]{:S(2)}) copy-start(bf16[512,1024]{1,0:T(8,128)(2,1)} %get-tuple-element.11) | copy-start | bytes 3145732

commit v4 on v3

--- a/solution.py
+++ b/solution.py
@@ -25,12 +25,15 @@
 FILL = -1e30
 MESH = pl.DeviceIdType.MESH
 CHUNKS = 8
-PER = HEADS // CHUNKS
+PER = 1
 STEP = 512
 
-IN_KV, IN_QG, COLUMN, BESIDE, ALONG, PAIR_SET, FROM_PREV = range(0, 7)
-FROM_NEXT, PAIR_GRAD, GRAD_PREV, GRAD_NEXT, ALONG_GRAD, BESIDE_GRAD, COLUMN_GRAD = range(7, 14)
-TRANSFERS = 14
+IN_KV, IN_QG, COLUMN, BESIDE, ALONG, ACROSS, PAIR_SET, FROM_PREV = range(0, 8)
+FROM_NEXT, PAIR_GRAD, GRAD_PREV, GRAD_NEXT, ALONG_GRAD, ACROSS_GRAD, BESIDE_GRAD, COLUMN_GRAD = range(8, 16)
+TRANSFERS = 16
+FORWARD = (IN_KV, IN_QG, COLUMN, BESIDE, ALONG, ACROSS, PAIR_SET, FROM_PREV, FROM_NEXT)
+PER_IN = 2
+LOADS = HEADS // PER_IN
 
 
 def dot_nt(a, b):
@@ -97,7 +100,7 @@
 
 def kernel(
     q_hbm, k_hbm, v_hbm, g_hbm, att, gq, gk, gv,
-    kv, q_all, g_all, pooled, told, heard, gown, gset, pair, csend, cin, csum, psend, pin, asend, ain,
+    kv, q_all, g_all, pooled, told, heard, gown, gset, pair, csend, clow, cline, cin, csum, psend, pin, asend, ain,
     tsend, tin, hrecv, bias, mean, spread, score, dprob, total,
     send, recv, small_send, small_recv,
 ):
@@ -107,6 +110,7 @@
     other = 1 - core
     sibling = (g, s + 1 - 2 * core)
     slot_one = x * 4 + high * 2 + core
+    across = ((1 - low) * 8 + z, s)
     has_prev = (g + s) > 0
     has_next = (g + s) < GROUPS + PLACES - 2
     up_group = lax.rem(g + lax.div(s + 1, PLACES), GROUPS)
@@ -132,8 +136,11 @@
     def one_rows(column, row, count):
         return ranks(LEVEL1 // ONE + column * 4 + row * 2, ONE, count)
 
-    def two_rows(column, row, count):
-        return ranks(LEVEL2 // ONE + column * 2 + row, ONE, count)
+    def two_rows(group, count):
+        return ranks(LEVEL2 // ONE + group, ONE, count)
+
+    def loads(ch):
+        return pl.ds(ch * PER_IN, PER_IN)
 
     def heads(ch):
         return pl.ds(ch * PER, PER)
@@ -148,14 +155,14 @@
         ).start()
 
     def await_rows(sems, transfer, ch, rows):
-        ref = kv.at[heads(ch), 0, pl.ds(0, rows), :]
+        ref = kv.at[loads(ch) if transfer in FORWARD else heads(ch), 0, pl.ds(0, rows), :]
         pltpu.make_async_copy(ref, ref, sems.at[transfer, ch]).wait()
 
     def each_head(ch, do):
         lax.fori_loop(0, PER, lambda i, _: (do(ch * PER + i), 0)[1], 0)
 
     def fetch(h, _):
-        ch = lax.div(h, PER)
+        ch = lax.div(h, PER_IN)
         for plane, src in enumerate((k_hbm, v_hbm)):
             pltpu.make_async_copy(
                 src.at[:, lanes(h)], kv.at[h, plane, pl.ds(OWN, BLOCK), :], recv.at[IN_KV, ch]
@@ -163,7 +170,7 @@
         return 0
 
     def fetch_more(h, _):
-        ch = lax.div(h, PER)
+        ch = lax.div(h, PER_IN)
         for dst, src in ((q_all, q_hbm), (g_all, g_hbm)):
             pltpu.make_async_copy(src.at[:, lanes(h)], dst.at[h], recv.at[IN_QG, ch]).start()
         return 0
@@ -176,17 +183,9 @@
     def meet(device):
         pl.semaphore_signal(barrier, inc=1, device_id=device, device_id_type=MESH)
 
-    def column_peer(j):
-        rank = lax.rem(low * PLACES + s + j, 2 * PLACES)
-        return lax.div(rank, PLACES), lax.rem(rank, PLACES)
-
-    def greet(j, _):
-        half, place = column_peer(j)
-        meet((half * 8 + z, place))
-        return 0
-
-    lax.fori_loop(1, 2 * PLACES, greet, 0)
+    lax.fori_loop(1, PLACES, lambda j, _: (meet((g, lax.rem(s + j, PLACES))), 0)[1], 0)
     lax.fori_loop(1, 8, lambda d, _: (meet(along(d)), 0)[1], 0)
+    meet(across)
     crosses_up = jnp.logical_and(s == PLACES - 1, has_next)
     crosses_down = jnp.logical_and(s == 0, has_prev)
 
@@ -204,9 +203,9 @@
     spread[...] = jnp.where(lax.shift_right_logical(tall[0], 4) == tall[1], 1.0 / POOL, 0.0).astype(BF16)
 
     def pool_own(h, _):
-        @pl.when(lax.rem(h, PER) == 0)
-        def _():
-            await_rows(recv, IN_KV, lax.div(h, PER), 2 * BLOCK)
+        @pl.when(lax.rem(h, PER_IN) == 0)
+        def _():
+            await_rows(recv, IN_KV, lax.div(h, PER_IN), 2 * BLOCK)
 
         for plane in range(2):
             pooled[plane, h] = dot_nn(mean[...], kv[h, plane, pl.ds(OWN, BLOCK), :]).astype(BF16)
@@ -215,7 +214,7 @@
 
     lax.fori_loop(0, HEADS, pool_own, 0)
     told[...] = dot_nn(mean[...], pooled[...].reshape(2 * HEADS * ONE, DIM)).astype(BF16)
-    heard[low * PLACES + slot_one] = told[...]
+    heard[slot_one] = told[...]
 
     @pl.when(jnp.logical_not(has_prev))
     def _():
@@ -231,22 +230,21 @@
 
     @pl.when(crosses)
     def _():
-        pl.semaphore_wait(barrier, 2 * PLACES - 1 + 7 + 1)
+        pl.semaphore_wait(barrier, PLACES - 1 + 8 + 1)
 
     @pl.when(jnp.logical_not(crosses))
     def _():
-        pl.semaphore_wait(barrier, 2 * PLACES - 1 + 7)
+        pl.semaphore_wait(barrier, PLACES - 1 + 8)
 
     def tell(j, _):
-        half, place = column_peer(j)
         pltpu.make_async_remote_copy(
-            src_ref=told, dst_ref=heard.at[low * PLACES + slot_one],
+            src_ref=told, dst_ref=heard.at[slot_one],
             send_sem=small_send.at[0], recv_sem=small_recv.at[0],
-            device_id=(half * 8 + z, place), device_id_type=MESH,
+            device_id=(g, lax.rem(s + j, PLACES)), device_id_type=MESH,
         ).start()
         return 0
 
-    lax.fori_loop(1, 2 * PLACES, tell, 0)
+    lax.fori_loop(1, PLACES, tell, 0)
 
     def await_small(sems, which, ref):
         pltpu.make_async_copy(ref, ref, sems.at[which]).wait()
@@ -260,38 +258,35 @@
         row = lax.broadcasted_iota(jnp.int32, (SET, DIM), 0)
         slot = lax.shift_right_logical(row & (BLOCK - 1), 5)
         place = (lax.shift_right_logical(slot, 1) & 1) * 8 + lax.shift_right_logical(slot, 2) * 2 + (slot & 1)
-        group = (slot & 1) * 8 + lax.shift_right_logical(slot, 1)
         dead_one = (row >= LEVEL1) & (row < LEVEL2) & (place >= s - 1) & (place <= s + 1)
-        dead_two = (row >= LEVEL2) & (group == g)
+        dead_two = (row >= LEVEL2) & (slot == g)
         no_prev = (row >= PREV) & (row < NEXT) & (g + s == 0)
         no_next = (row >= NEXT) & (row < LEVEL1) & (g + s == GROUPS + PLACES - 2)
         bias[...] = jnp.where(dead_one | dead_two | no_prev | no_next, FILL, 0.0)
 
     def own_coarse():
-        await_small(small_recv, 0, heard.at[pl.ds(0, 2 * PLACES - 1)])
+        await_small(small_recv, 0, heard.at[pl.ds(0, PLACES - 1)])
         shape = (HEADS * ONE, PLACES * ONE)
         to, come = lax.broadcasted_iota(jnp.int32, shape, 0), lax.broadcasted_iota(jnp.int32, shape, 1)
         head, within = lax.shift_right_logical(to, 5), to & 31
         wanted = lax.shift_right_logical(within, 1) * ONE + core * 16 + head * 2 + (within & 1)
         pick = jnp.where(come == wanted, 1.0, 0.0).astype(BF16)
-        for half in range(2):
-            there = heard[half * PLACES : (half + 1) * PLACES].reshape(PLACES * ONE, DIM)
-            rows = dot_nn(pick, there).astype(BF16)
-            for h in range(HEADS):
-                kv[h, core, two_rows(z, half, ONE), :] = rows[h * ONE : (h + 1) * ONE]
+        rows = dot_nn(pick, heard[...].reshape(PLACES * ONE, DIM)).astype(BF16)
+        for h in range(HEADS):
+            kv[h, core, two_rows(g, ONE), :] = rows[h * ONE : (h + 1) * ONE]
 
     def column(which):
         return (g, (1 - high) * 8 + x * 2 + which)
 
     def send_column(ch):
-        hs = heads(ch)
+        hs = loads(ch)
         mine = ranks(LEVEL1 // ONE + slot_one, ONE, ONE)
         for plane in range(2):
             push(COLUMN, ch, pooled.at[plane, hs], kv.at[hs, plane, mine, :], column(plane))
         push(COLUMN, ch, pooled.at[other, hs], kv.at[hs, other, mine, :], sibling)
 
     def send_planes(ch):
-        hs = heads(ch)
+        hs = loads(ch)
         await_rows(recv, COLUMN, ch, 3 * ONE)
         rows = kv.at[hs, core, one_rows(x, 0, 4 * ONE), :]
         for d in (2, 1, 3):
@@ -301,9 +296,9 @@
         def _():
             own_coarse()
 
-        both = kv.at[hs, core, two_rows(z, 0, 2 * ONE), :]
+        group = kv.at[hs, core, two_rows(g, ONE), :]
         for d in (4, 3, 5, 2, 6, 1, 7):
-            push(ALONG, ch, both, both, along(d))
+            push(ALONG, ch, group, group, along(d))
 
         @pl.when(has_next)
         def _():
@@ -317,26 +312,35 @@
         def _():
             tables()
 
+    def send_across(ch):
+        hs = loads(ch)
+        await_rows(recv, ALONG, ch, 7 * ONE)
+        line = kv.at[hs, core, two_rows(low * 8, 8 * ONE), :]
+        push(ACROSS, ch, line, line, across)
+
     def swap_set(ch):
-        hs = heads(ch)
+        hs = loads(ch)
         await_rows(recv, BESIDE, ch, 12 * ONE)
-        await_rows(recv, ALONG, ch, 14 * ONE)
+        await_rows(recv, ACROSS, ch, 8 * ONE)
         whole = kv.at[hs, core, pl.ds(LEVEL1, 2 * BLOCK), :]
         push(PAIR_SET, ch, whole, whole, sibling)
 
+    def await_set(ch):
+        await_rows(recv, IN_QG, ch, 2 * BLOCK)
+        await_rows(recv, PAIR_SET, ch, 2 * BLOCK)
+
+        @pl.when(has_prev)
+        def _():
+            await_rows(recv, FROM_PREV, ch, 2 * NEAR)
+
+        @pl.when(has_next)
+        def _():
+            await_rows(recv, FROM_NEXT, ch, 2 * NEAR)
+
     def compute(ch):
         hs = heads(ch)
-        await_rows(recv, IN_QG, ch, 2 * BLOCK)
-        await_rows(recv, PAIR_SET, ch, 2 * BLOCK)
-
-        @pl.when(has_prev)
-        def _():
-            await_rows(recv, FROM_PREV, ch, 2 * NEAR)
-
-        @pl.when(has_next)
-        def _():
-            await_rows(recv, FROM_NEXT, ch, 2 * NEAR)
-
+        ready = lax.div(ch, PER_IN)
+        pl.when(lax.rem(ch, PER_IN) == 0)(functools.partial(await_set, ready))
         each_head(
             ch,
             lambda h: attend(h, q_all, g_all, kv, bias, att, gq, gown, gset, score, dprob, total),
@@ -368,11 +372,9 @@
                 BESIDE_GRAD, ch, psend.at[hs, ranks(near_x(d), 128, 128), :],
                 pin.at[hs, ranks(x, 128, 128), :], beside(d),
             )
-        for d in (4, 3, 5, 2, 6, 1, 7):
-            push(
-                ALONG_GRAD, ch, csend.at[hs, ranks(near_z(d), 64, 64), :],
-                cin.at[hs, ranks(z, 64, 64), :], along(d),
-            )
+        push(
+            ACROSS_GRAD, ch, csend.at[hs, ranks((1 - low) * 8, ONE, 8 * ONE), :], clow.at[hs], across,
+        )
 
     def column_grads(ch):
         hs = heads(ch)
@@ -393,15 +395,28 @@
                 column(which),
             )
         push(COLUMN_GRAD, ch, asend.at[hs, ranks(high * 2 + other, ONE, ONE), :], place, sibling)
-        await_rows(recv, ALONG_GRAD, ch, 14 * ONE)
-
-        def add_coarse(h):
-            v = csend[h, ranks(z, 64, 64), :].astype(F32)
+        await_rows(recv, ACROSS_GRAD, ch, 8 * ONE)
+
+        def add_line(h):
+            cline[h] = added(csend[h, ranks(low * 8, ONE, 8 * ONE), :], clow[h])
+
+        each_head(ch, add_line)
+        for d in (4, 3, 5, 2, 6, 1, 7):
+            push(
+                ALONG_GRAD, ch, cline.at[hs, ranks(near_z(d), ONE, ONE), :],
+                cin.at[hs, ranks(z, ONE, ONE), :], along(d),
+            )
+
+    def coarse_sums(ch):
+        await_rows(recv, ALONG_GRAD, ch, 7 * ONE)
+
+        def add(h):
+            v = cline[h, ranks(z, ONE, ONE), :].astype(F32)
             for d in range(1, 8):
-                v = v + cin[h, ranks(near_z(d), 64, 64), :].astype(F32)
+                v = v + cin[h, ranks(near_z(d), ONE, ONE), :].astype(F32)
             csum[h] = v.astype(BF16)
 
-        each_head(ch, add_coarse)
+        each_head(ch, add)
 
     def finish(ch):
         await_rows(recv, COLUMN_GRAD, ch, 3 * ONE)
@@ -425,47 +440,49 @@
 
         each_head(ch, add)
 
-    stages = (send_column, send_planes, swap_set, compute, send_grads, column_grads, finish)
+    inward = (send_column, send_planes, send_across, swap_set)
+    outward = (compute, send_grads, column_grads, coarse_sums, finish)
+    lead = len(inward) - 1
 
     def step(t, _):
-        for lag, stage in enumerate(stages):
+        for lag, stage in enumerate(inward):
+            pl.when(jnp.logical_and(t >= lag, t < LOADS + lag))(functools.partial(stage, t - lag))
+        for i, stage in enumerate(outward):
+            lag = lead + 1 + i
             pl.when(jnp.logical_and(t >= lag, t < CHUNKS + lag))(functools.partial(stage, t - lag))
-
-        @pl.when(t == CHUNKS + 4)
-        def _():
-            send_coarse_sums()
-
+            if stage is coarse_sums:
+                pl.when(t == CHUNKS + lag - 1)(send_coarse_sums)
         return 0
 
     def send_coarse_sums():
-        shape = (BLOCK, BLOCK)
+        shape = (HEADS * ONE, HEADS * ONE)
         to, come = lax.broadcasted_iota(jnp.int32, shape, 0), lax.broadcasted_iota(jnp.int32, shape, 1)
         target, within = lax.shift_right_logical(to, 4), to & 15
-        wanted = lax.shift_right_logical(within, 1) * 64 + target * 2 + (within & 1)
+        wanted = lax.shift_right_logical(within, 1) * ONE + target * 2 + (within & 1)
         pick = jnp.where(come == wanted, 1.0, 0.0).astype(BF16)
-        tsend[...] = dot_nn(pick, csum[...].reshape(BLOCK, DIM)).astype(BF16)
-        source = low * 8 + high * 4 + x
-        tin[core, source] = tsend[ranks(low * PLACES + slot_one, 16, 16), :]
+        tsend[...] = dot_nn(pick, csum[...].reshape(HEADS * ONE, DIM)).astype(BF16)
+        source = high * 4 + x
+        tin[core, source] = tsend[ranks(slot_one, 16, 16), :]
 
         def tell_sums(j, _):
-            half, place = column_peer(j)
+            place = lax.rem(s + j, PLACES)
             slot = lax.div(lax.rem(place, 8), 2) * 4 + lax.div(place, 8) * 2 + lax.rem(place, 2)
             pltpu.make_async_remote_copy(
-                src_ref=tsend.at[ranks(half * PLACES + slot, 16, 16), :], dst_ref=tin.at[core, source],
+                src_ref=tsend.at[ranks(slot, 16, 16), :], dst_ref=tin.at[core, source],
                 send_sem=small_send.at[1], recv_sem=small_recv.at[1],
-                device_id=(half * 8 + z, place), device_id_type=MESH,
+                device_id=(g, place), device_id_type=MESH,
             ).start()
             return 0
 
-        lax.fori_loop(1, 2 * PLACES, tell_sums, 0)
-
-    lax.fori_loop(0, CHUNKS + len(stages) - 1, step, 0)
-
-    sums_in = tsend.at[pl.ds(0, (2 * PLACES - 1) * 16), :]
+        lax.fori_loop(1, PLACES, tell_sums, 0)
+
+    lax.fori_loop(0, CHUNKS + lead + len(outward), step, 0)
+
+    sums_in = tsend.at[pl.ds(0, (PLACES - 1) * 16), :]
     await_small(small_recv, 1, sums_in)
     for plane, dst in enumerate((gk, gv)):
         coarse = tin[plane, 0].astype(F32)
-        for i in range(1, 16):
+        for i in range(1, 8):
             coarse = coarse + tin[plane, i].astype(F32)
         coarse = coarse * (1.0 / (POOL * POOL))
         for h in range(HEADS):
@@ -474,33 +491,31 @@
                 row = coarse[2 * h + side : 2 * h + side + 1]
                 dst[rows, h * DIM : (h + 1) * DIM] = (gown[h, plane, rows, :] + row).astype(BF16)
 
-    await_small(small_send, 0, heard.at[pl.ds(0, 2 * PLACES - 1)])
+    await_small(small_send, 0, heard.at[pl.ds(0, PLACES - 1)])
     await_small(small_send, 1, sums_in)
 
     def drain(ch, _):
         for transfer, rows in (
-            (COLUMN, 96), (BESIDE, 384), (ALONG, 448), (PAIR_SET, 1024),
-            (PAIR_GRAD, 1024), (ALONG_GRAD, 448), (BESIDE_GRAD, 384), (COLUMN_GRAD, 96),
+            (PAIR_GRAD, 1024), (ACROSS_GRAD, 256), (ALONG_GRAD, 224), (BESIDE_GRAD, 384), (COLUMN_GRAD, 96),
         ):
             await_rows(send, transfer, ch, rows)
-
-        @pl.when(has_prev)
-        def _():
-            await_rows(send, FROM_NEXT, ch, 2 * NEAR)
-            await_rows(send, GRAD_NEXT, ch, 2 * NEAR)
-
-        @pl.when(has_next)
-        def _():
-            await_rows(send, FROM_PREV, ch, 2 * NEAR)
-            await_rows(send, GRAD_PREV, ch, 2 * NEAR)
-
-        return 0
-
+        pl.when(has_prev)(lambda: await_rows(send, GRAD_NEXT, ch, 2 * NEAR))
+        pl.when(has_next)(lambda: await_rows(send, GRAD_PREV, ch, 2 * NEAR))
+        return 0
+
+    def drain_in(ch, _):
+        for transfer, rows in ((COLUMN, 96), (BESIDE, 384), (ALONG, 224), (ACROSS, 256), (PAIR_SET, 1024)):
+            await_rows(send, transfer, ch, rows)
+        pl.when(has_prev)(lambda: await_rows(send, FROM_NEXT, ch, 2 * NEAR))
+        pl.when(has_next)(lambda: await_rows(send, FROM_PREV, ch, 2 * NEAR))
+        return 0
+
+    lax.fori_loop(0, LOADS, drain_in, 0)
     lax.fori_loop(0, CHUNKS, drain, 0)
 
 
 def body(query_rows, key_rows, value_rows, grad_out):
-    shape = jax.ShapeDtypeStruct(query_rows.shape, BF16)
+    shape = pltpu.VMEM(query_rows.shape, BF16)
 
     def rows(count, *lead):
         return ((*lead, HEADS, count, DIM), BF16)
@@ -511,19 +526,21 @@
         rows(BLOCK),
         rows(ONE, 2),
         ((ONE, DIM), BF16),
-        ((2 * PLACES, ONE, DIM), BF16),
+        ((PLACES, ONE, DIM), BF16),
         ((HEADS, 2, BLOCK, DIM), F32),
         ((HEADS, 2, SET - BLOCK, DIM), BF16),
         rows(2 * BLOCK),
         rows(BLOCK),
-        rows(BLOCK),
-        rows(64),
+        rows(8 * ONE),
+        rows(8 * ONE),
+        rows(8 * ONE),
+        rows(ONE),
         rows(BLOCK),
         rows(BLOCK),
         rows(128),
         rows(128),
-        ((BLOCK, DIM), BF16),
-        ((2, 16, 16, DIM), BF16),
+        ((HEADS * ONE, DIM), BF16),
+        ((2, 8, 16, DIM), BF16),
         ((HEADS, 2, 2, NEAR, DIM), BF16),
         ((SET, DIM), F32),
         ((ONE, BLOCK), BF16),
@@ -542,7 +559,7 @@
         + [pltpu.SemaphoreType.DMA((TRANSFERS, CHUNKS))] * 2
         + [pltpu.SemaphoreType.DMA((2,))] * 2,
         compiler_params=pltpu.CompilerParams(
-            collective_id=0, has_side_effects=True, vmem_limit_bytes=58 << 20
+            collective_id=0, has_side_effects=True, vmem_limit_bytes=50 << 20
         ),
         name="hierarchical",
     )(query_rows, key_rows, value_rows, grad_out)

time: 110 us -> 103 us (0.936)
  Pallas kernels: 102 us -> 98.4 us
  local copies, waits for them, and re-layouts: 6.53 us -> 3.88 us
    pallas_call x1, Pallas kernels: 102 us -> 98.4 us  [body(): pl.pallas_call(kernel, out_shape=[shape] * 4, in_specs=[anywhere] * 4, ou...]
    unnamed x10 -> x4, local copies, waits for them, and re-layouts: 6.53 us -> 3.88 us
where the time goes in v4:
time: 103 us
  Pallas kernels  98.4 us (96%)
  local copies, waits for them, and re-layouts  3.88 us (4%)
    pallas_call x1, Pallas kernels, body(): pl.pallas_call(kernel, out_shape=[shape] * 4, in_specs=[anywhere] * 4, ou...  98.4 us
    unnamed x4, local copies, waits for them, and re-layouts  3.88 us

profile of v4, /device:TPU:1, one launch (start us, length us, event | category | flops | bytes accessed | tf_op | source)
XLA Modules:
  0.0 102.9 jit_solution(12434982249245744172)
XLA Ops:
  0.6 98.4 %hierarchical.1 = (bf16[512,1024]{1,0:T(8,128)(2,1)S(1)}, bf16[512,1024]{1,0:T(8,128)(2,1)S(1)}, bf16[512,1024]{1,0:T(8,128)(2,1)S(1)}, bf16[512,1024]{1,0:T(8,128)(2,1)S(1)}) custom-call(bf16[512,1024]{1,0:T(8,128)(2,1)} %q_hbm.1, bf16[512,1024]{1,0:T(8,128)(2,1)} %k_hbm.1, bf16[512,1024]{1,0:T(8,128)(2,1)} %v_hbm.1, bf16[512,1024]{1,0:T(8,128)(2,1)} %g_hbm.1), custom_call_target="tpu_custom_call" | custom-call | tf_op jit(solution)/shard_map/hierarchical/pallas_call | solution.py:553
  99.1 1.0 copy.12
  100.0 1.0 copy.13
  101.0 1.0 copy.14
  102.0 1.0 copy.15

commit v5 on v4

--- a/solution.py
+++ b/solution.py
@@ -32,7 +32,7 @@
 FROM_NEXT, PAIR_GRAD, GRAD_PREV, GRAD_NEXT, ALONG_GRAD, ACROSS_GRAD, BESIDE_GRAD, COLUMN_GRAD = range(8, 16)
 TRANSFERS = 16
 FORWARD = (IN_KV, IN_QG, COLUMN, BESIDE, ALONG, ACROSS, PAIR_SET, FROM_PREV, FROM_NEXT)
-PER_IN = 2
+PER_IN = 1
 LOADS = HEADS // PER_IN
 
 
@@ -445,13 +445,17 @@
     lead = len(inward) - 1
 
     def step(t, _):
-        for lag, stage in enumerate(inward):
-            pl.when(jnp.logical_and(t >= lag, t < LOADS + lag))(functools.partial(stage, t - lag))
-        for i, stage in enumerate(outward):
-            lag = lead + 1 + i
+        pl.when(jnp.logical_and(t >= lead + 1, t < CHUNKS + lead + 1))(lambda: compute(t - lead - 1))
+        for i, stage in enumerate(outward[1:]):
+            lag = lead + 2 + i
             pl.when(jnp.logical_and(t >= lag, t < CHUNKS + lag))(functools.partial(stage, t - lag))
             if stage is coarse_sums:
                 pl.when(t == CHUNKS + lag - 1)(send_coarse_sums)
+        for lag, stage in enumerate(inward):
+            first, last = 2 * (t - lag) - 1, 2 * (t - lag) + 1
+            lax.fori_loop(
+                jnp.maximum(first, 0), jnp.minimum(last, LOADS), lambda ch, _: (stage(ch), 0)[1], 0
+            )
         return 0
 
     def send_coarse_sums():

time: 103 us -> 99.1 us (0.962)
  Pallas kernels: 98.4 us -> 94.5 us
    pallas_call x1, Pallas kernels: 98.4 us -> 94.5 us  [body(): pl.pallas_call(kernel, out_shape=[shape] * 4, in_specs=[anywhere] * 4, ou...]
where the time goes in v5:
time: 99.1 us; the launch traced here: 99 us
  Pallas kernels  94.5 us (95%)
  local copies, waits for them, and re-layouts  3.88 us (4%)
    pallas_call x1, Pallas kernels, body(): pl.pallas_call(kernel, out_shape=[shape] * 4, in_specs=[anywhere] * 4, ou...  94.5 us
    unnamed x4, local copies, waits for them, and re-layouts  3.88 us

profile of v5, /device:TPU:1, one launch (start us, length us, event | category | flops | bytes accessed | tf_op | source)
XLA Modules:
  0.0 99.0 jit_solution(7269918216402238715)
XLA Ops:
  0.6 94.5 %hierarchical.1 = (bf16[512,1024]{1,0:T(8,128)(2,1)S(1)}, bf16[512,1024]{1,0:T(8,128)(2,1)S(1)}, bf16[512,1024]{1,0:T(8,128)(2,1)S(1)}, bf16[512,1024]{1,0:T(8,128)(2,1)S(1)}) custom-call(bf16[512,1024]{1,0:T(8,128)(2,1)} %q_hbm.1, bf16[512,1024]{1,0:T(8,128)(2,1)} %k_hbm.1, bf16[512,1024]{1,0:T(8,128)(2,1)} %v_hbm.1, bf16[512,1024]{1,0:T(8,128)(2,1)} %g_hbm.1), custom_call_target="tpu_custom_call" | custom-call | tf_op jit(solution)/shard_map/hierarchical/pallas_call | solution.py:557
  95.1 1.0 copy.12
  96.1 1.0 copy.13
  97.1 1.0 copy.14
  98.0 1.0 copy.15

commit v6 on v5

--- a/solution.py
+++ b/solution.py
@@ -285,6 +285,14 @@
             push(COLUMN, ch, pooled.at[plane, hs], kv.at[hs, plane, mine, :], column(plane))
         push(COLUMN, ch, pooled.at[other, hs], kv.at[hs, other, mine, :], sibling)
 
+        @pl.when(has_next)
+        def _():
+            push(FROM_PREV, ch, kv.at[hs, :, pl.ds(OWN + BLOCK - NEAR, NEAR), :], kv.at[hs, :, pl.ds(PREV, NEAR), :], after)
+
+        @pl.when(has_prev)
+        def _():
+            push(FROM_NEXT, ch, kv.at[hs, :, pl.ds(OWN, NEAR), :], kv.at[hs, :, pl.ds(NEXT, NEAR), :], before)
+
     def send_planes(ch):
         hs = loads(ch)
         await_rows(recv, COLUMN, ch, 3 * ONE)
@@ -299,14 +307,6 @@
         group = kv.at[hs, core, two_rows(g, ONE), :]
         for d in (4, 3, 5, 2, 6, 1, 7):
             push(ALONG, ch, group, group, along(d))
-
-        @pl.when(has_next)
-        def _():
-            push(FROM_PREV, ch, kv.at[hs, :, pl.ds(OWN + BLOCK - NEAR, NEAR), :], kv.at[hs, :, pl.ds(PREV, NEAR), :], after)
-
-        @pl.when(has_prev)
-        def _():
-            push(FROM_NEXT, ch, kv.at[hs, :, pl.ds(OWN, NEAR), :], kv.at[hs, :, pl.ds(NEXT, NEAR), :], before)
 
         @pl.when(ch == 0)
         def _():

time: 99.1 us -> 102 us (1.029)
  Pallas kernels: 94.5 us -> 97.8 us
    pallas_call x1, Pallas kernels: 94.5 us -> 97.8 us  [body(): pl.pallas_call(kernel, out_shape=[shape] * 4, in_specs=[anywhere] * 4, ou...]
where the time goes in v6:
time: 102 us
  Pallas kernels  97.8 us (96%)
  local copies, waits for them, and re-layouts  3.88 us (4%)
    pallas_call x1, Pallas kernels, body(): pl.pallas_call(kernel, out_shape=[shape] * 4, in_specs=[anywhere] * 4, ou...  97.8 us
    unnamed x4, local copies, waits for them, and re-layouts  3.88 us

profile of v6, /device:TPU:1, one launch (start us, length us, event | category | flops | bytes accessed | tf_op | source)
XLA Modules:
  0.0 102.3 jit_solution(6614426919126875487)
XLA Ops:
  0.6 97.8 %hierarchical.1 = (bf16[512,1024]{1,0:T(8,128)(2,1)S(1)}, bf16[512,1024]{1,0:T(8,128)(2,1)S(1)}, bf16[512,1024]{1,0:T(8,128)(2,1)S(1)}, bf16[512,1024]{1,0:T(8,128)(2,1)S(1)}) custom-call(bf16[512,1024]{1,0:T(8,128)(2,1)} %q_hbm.1, bf16[512,1024]{1,0:T(8,128)(2,1)} %k_hbm.1, bf16[512,1024]{1,0:T(8,128)(2,1)} %v_hbm.1, bf16[512,1024]{1,0:T(8,128)(2,1)} %g_hbm.1), custom_call_target="tpu_custom_call" | custom-call | tf_op jit(solution)/shard_map/hierarchical/pallas_call | solution.py:557
  98.4 1.0 copy.12
  99.4 1.0 copy.13
  100.3 1.0 copy.14
  101.3 1.0 copy.15
